TPU v7x, 256 devices: a whole 4x4x8 slice. The times are simulated.
256 devices in a mesh: lon: 32 (over z, y), lat: 8 (over x, core).
Axes of the slice: x: 4, y: 4, z: 8, core: 2. Of those that a mesh axis runs over, the one named last changes fastest.
Arguments:
- fields: float32 [6, 128, 8, 32768], P(None, None, 'lat', 'lon'), may hold values from -6 to 6
- sunlit: int32 [8, 32768], P('lat', 'lon'), may hold values from 0 to 1, as said below
- w_in: bfloat16 [64, 768], replicated, may hold values from -0.21875 to 0.21875
- b_in: float32 [64], replicated, may hold values from -3 to 3
- w_out: bfloat16 [224, 64], replicated, may hold values from -0.75 to 0.75
- b_out: float32 [224], replicated, may hold values from -4 to 4
- level_map: float32 [128, 224], replicated, may hold values from -24 to 24
- dep_owner: int32 [8, 8192, 1], P('lat', 'lon'), may hold values from 0 to 255; in each aligned block of 256 rows (0 to 255, 256 to 511, ..., all dimensions but the last counted through in order) at most 2 rows name the same one
- owner_unit: int32 [8, 8192], P('lat', 'lon'), may hold values from 0 to 255
- h_frac: float32 [8, 8192, 128], P('lat', 'lon'), may hold values from 0 to 1
- h_shift: int32 [8, 8192, 128], P('lat', 'lon'), may hold values from -3 to 3
- v_frac: float32 [8, 256, 128], P('lat', 'lon'), may hold values from 0 to 1
- v_shift: int32 [8, 256, 128], P('lat', 'lon'), may hold values from -2 to 2
Outputs:
- advected: float32 [6, 128, 8, 32768], P(None, None, 'lat', 'lon')
- heating: float32 [128, 8, 32768], P(None, 'lat', 'lon')
Inputs may be any that keep to these rules, and one draw needn't show every extreme that they name: At each latitude the sunlit columns form one run, contiguous modulo 32768, of 8192 to 24576 columns, starting at the same column at every latitude. `dep_owner`: the 256 units of one device name no owner more than 2 times, and some device names some owner exactly 2 times.
All inputs are finite; a program needn't handle non-finite values.
Results may differ from a plain program's by a relative error of at most 0.0015.
Values may be sent and summed in bfloat16 or wider, within the bound.
No kernel may reach another device: no remote copies, remote signals or barrier semaphores. Data moves between devices by JAX's collectives and lax.ppermute only.
A program may use at most 128 MiB of HBM per device.

v0:
```python
import math

import jax
import jax.numpy as jnp
from jax import lax
from jax.sharding import PartitionSpec as P

BLOCK = 128
LG = 4


def from_partner(value, axis, distance):
    mask = 2**distance
    pairs = [(source, source ^ mask) for source in range(lax.axis_size(axis))]
    return lax.ppermute(value, axis, pairs)


def cubic_weights(fraction):
    return (
        -fraction * (fraction - 1.0) * (fraction - 2.0) / 6.0,
        (fraction + 1.0) * (fraction - 1.0) * (fraction - 2.0) / 2.0,
        -(fraction + 1.0) * fraction * (fraction - 2.0) / 2.0,
        (fraction + 1.0) * fraction * (fraction - 1.0) / 6.0,
    )


def interp_matrix(fraction, displace, length):
    col_count = fraction.shape[-1]
    position = jnp.arange(col_count, dtype=jnp.int32)
    source = jnp.arange(length, dtype=jnp.int32)[:, None]
    weights = cubic_weights(fraction)
    summed = jnp.zeros(fraction.shape[:-1] + (length, col_count), jnp.float32)
    for offset in range(4):
        stencil = jnp.clip(position + displace + (offset - 1), 0, length - 1)
        summed = summed + weights[offset][..., None, :] * (source == stencil[..., None, :]).astype(
            jnp.float32
        )
    return summed


def column_heating(features, lit_mask, network):
    w_in, b_in, w_out, b_out, level_map = network
    out_count = w_out.shape[0]
    rows_idx = jnp.arange(out_count, dtype=jnp.int32)
    lower_ones = (rows_idx[:, None] >= rows_idx[None, :]).astype(jnp.float32)
    hidden = jnp.tanh(
        jnp.dot(w_in, features, preferred_element_type=jnp.float32) + b_in[:, None]
    ).astype(jnp.bfloat16)
    optical = jax.nn.softplus(
        jnp.dot(w_out, hidden, preferred_element_type=jnp.float32) + b_out[:, None]
    ) * (4.0 / out_count)
    column_depth = jnp.dot(lower_ones, optical, precision=lax.Precision.HIGHEST)
    absorbed = optical * jnp.exp(-column_depth)
    return jnp.dot(level_map, absorbed, precision=lax.Precision.HIGHEST) * lit_mask[None, :]


def heat_all(features, lit_mask, network):
    levels = network[4].shape[0]
    blocks_n = features.shape[1] // BLOCK

    def one_block(block_number):
        offset_row = block_number * BLOCK
        feature_block = lax.dynamic_slice_in_dim(features, offset_row, BLOCK, 1)
        lit_block = lax.dynamic_slice_in_dim(lit_mask, offset_row, BLOCK, 0)
        return lax.cond(
            jnp.any(lit_block > 0),
            lambda: column_heating(feature_block, lit_block, network),
            lambda: jnp.zeros((levels, BLOCK), jnp.float32),
        )

    stacked = lax.map(one_block, jnp.arange(blocks_n, dtype=jnp.int32))
    return stacked.transpose(1, 0, 2).reshape(levels, blocks_n * BLOCK)


def per_device(
    fields,
    sunlit,
    w_in,
    b_in,
    w_out,
    b_out,
    level_map,
    dep_owner,
    owner_unit,
    h_frac,
    h_shift,
    v_frac,
    v_shift,
):
    network = (w_in, b_in, w_out, b_out, level_map)
    n_fields = fields.shape[0]
    levels = fields.shape[1]
    columns = fields.shape[3]
    column_state = fields[:, :, 0, :]
    lon_n = lax.axis_size("lon")
    lat_n = lax.axis_size("lat")
    devices_n = lon_n * lat_n
    units_n = owner_unit.shape[1]
    blocks_n = columns // BLOCK
    groups_n = levels // LG
    slot_count = max(1, 2 * units_n // devices_n)
    owners = dep_owner[0, :, 0]
    owner_marks = (owners[:, None] == jnp.arange(devices_n, dtype=jnp.int32)[None, :]).astype(
        jnp.int32
    )
    slot_rank = jnp.sum((jnp.cumsum(owner_marks, axis=0) - 1) * owner_marks, axis=1)
    landing = owners * slot_count + slot_rank
    wanted = jnp.full((devices_n * slot_count,), -1, jnp.int32).at[landing].set(owner_unit[0])
    asked_for = lax.all_to_all(
        lax.all_to_all(
            wanted.reshape(lat_n, lon_n, slot_count), "lon", split_axis=1, concat_axis=1, tiled=True
        ),
        "lat",
        split_axis=0,
        concat_axis=0,
        tiled=True,
    )
    picked = jnp.clip(asked_for.reshape(-1), 0, units_n - 1)
    features = column_state.reshape(n_fields * levels, columns).astype(jnp.bfloat16)
    lit_mask = sunlit[0]
    swap_bit = lon_n.bit_length() - 2
    half_cols = columns // 2
    column_pairs = features.reshape(n_fields * levels, half_cols, 2)
    lit_pairs = lit_mask.astype(jnp.bfloat16).reshape(half_cols, 2)
    got_features, got_lit = from_partner((column_pairs[:, :, 1], lit_pairs[:, 1]), "lon", swap_bit)
    mixed_heat = heat_all(
        jnp.concatenate([column_pairs[:, :, 0], got_features], axis=1),
        jnp.concatenate([lit_pairs[:, 0], got_lit], axis=0).astype(jnp.float32),
        network,
    )
    returned = from_partner(mixed_heat[:, half_cols:], "lon", swap_bit)
    heating = jnp.stack([mixed_heat[:, :half_cols], returned], axis=-1).reshape(levels, columns)
    warmed = column_state[0] + heating
    all_fields = jnp.concatenate([warmed[None], column_state[1:]], axis=0)
    n_items = all_fields.shape[0]
    sectioned = all_fields.reshape(n_items, groups_n, LG, blocks_n, BLOCK).transpose(1, 3, 0, 2, 4)
    unit_data = sectioned.reshape(units_n, n_items, LG, BLOCK)
    arrived = lax.all_to_all(
        lax.all_to_all(
            unit_data[picked].reshape(lat_n, lon_n, slot_count, unit_data.shape[1], LG, BLOCK),
            "lon",
            split_axis=1,
            concat_axis=1,
            tiled=True,
        ),
        "lat",
        split_axis=0,
        concat_axis=0,
        tiled=True,
    )
    sources = arrived.reshape(devices_n * slot_count, arrived.shape[3], LG, BLOCK)[landing]
    frac_cols = h_frac[0]
    shift_cols = h_shift[0]
    group_size = math.gcd(units_n, 16)

    def trace_group(group_number):
        offset_row = group_number * group_size
        source_rows = lax.dynamic_slice_in_dim(sources, offset_row, group_size, 0)
        matrix = interp_matrix(
            lax.dynamic_slice_in_dim(frac_cols, offset_row, group_size, 0),
            lax.dynamic_slice_in_dim(shift_cols, offset_row, group_size, 0),
            BLOCK,
        )
        return jnp.einsum("ufgr,urc->ufgc", source_rows, matrix, precision=lax.Precision.HIGHEST)

    traced = lax.map(trace_group, jnp.arange(units_n // group_size, dtype=jnp.int32))
    traced = traced.reshape(groups_n, blocks_n, n_fields, LG, BLOCK)
    regrid = traced.transpose(2, 0, 3, 1, 4).reshape(n_fields, levels, blocks_n, BLOCK)
    vertical = interp_matrix(v_frac[0], v_shift[0], levels)
    advected = jnp.einsum("blk,flbc->fkbc", vertical, regrid, precision=lax.Precision.HIGHEST)
    return (advected.reshape(n_fields, levels, 1, columns), heating.reshape(levels, 1, columns))


def solution(mesh):
    placed = (
        P(None, None, "lat", "lon"),
        P("lat", "lon"),
        P(),
        P(),
        P(),
        P(),
        P(),
        P("lat", "lon", None),
        P("lat", "lon"),
        P("lat", "lon", None),
        P("lat", "lon", None),
        P("lat", "lon", None),
        P("lat", "lon", None),
    )
    return jax.shard_map(
        per_device,
        mesh=mesh,
        in_specs=placed,
        out_specs=(P(None, None, "lat", "lon"), P(None, "lat", "lon")),
        check_vma=False,
    )
```

profile of v0, /device:TPU:1, one launch (start us, length us, event | category | flops | bytes accessed | tf_op | source)
XLA Modules:
  0.0 496.6 jit_solution(6753936227791794199)
XLA Ops:
  0.6 4.0 convert_element_type.42
  4.7 5.2 %copy.140 = bf16[6,128,1,1024]{1,0,3,2:T(8,128)(2,1)} copy(bf16[6,128,1,1024]{3,2,1,0:T(2,128)(2,1)S(1)} %convert_element_type.42) | data formatting | bytes 3145728 | tf_op jit(solution)/shard_map/convert_element_type | solution.py:119
  9.9 3.7 convert_element_type.43
  13.6 3.1 fusion.90
  16.7 3.5 copy.142
  20.1 7.8 %collective-permute-start.1 = (bf16[768,512]{1,0:T(8,128)(2,1)S(1)}, bf16[768,512]{1,0:T(8,128)(2,1)}, u32[]{:S(2)}, u32[]{:S(2)}) collective-permute-start(bf16[768,512]{1,0:T(8,128)(2,1)S(1)} %bitcast.129), channel_id=1, source_target_pairs={{0,128},{8,136},{16,144},{24,152},{32,160},{40,168},{48,176},{56,1... | collective-permute-start | bytes 2359304 | tf_op jit(solution)/shard_map/ppermute | solution.py:15
  28.7 1.6 scatter_custom_fusion
  30.4 0.9 copy.152
  31.3 5.9 %all-to-all-start = ((s32[8,32,2]{0,2,1:T(2,128)}), s32[8,32,2]{0,2,1:T(2,128)S(1)}, u32[]{:S(2)}, u32[]{:S(2)}) async-start(s32[8,32,2]{0,2,1:T(2,128)} %copy.152), calls=%async_computation | async-start | bytes 65536 | tf_op jit(solution)/shard_map/all_to_all | solution.py:110
  37.7 5.2 %collective-permute-start = (bf16[512]{0:T(512)(128)(2,1)S(1)}, bf16[512]{0:T(512)(128)(2,1)S(1)}, u32[]{:S(2)}, u32[]{:S(2)}) collective-permute-start(bf16[512]{0:T(512)(128)(2,1)S(1)} %get-tuple-element.299), channel_id=1, source_target_pairs={{0,128},{8,136},{16,144},{24,152},{32,160},{40,168},{48,176},{56,1... | collective-permute-start | bytes 3080 | tf_op jit(solution)/shard_map/ppermute | solution.py:15
  43.0 3.3 copy.141
  46.5 20.0 %all-to-all-done = s32[8,32,2]{0,2,1:T(2,128)S(1)} async-done(((s32[8,32,2]{0,2,1:T(2,128)}), s32[8,32,2]{0,2,1:T(2,128)S(1)}, u32[]{:S(2)}, u32[]{:S(2)}) %all-to-all-start) | async-done | bytes 2080 | tf_op jit(solution)/shard_map/all_to_all | solution.py:110
  67.2 5.2 %all-to-all-start.1 = ((s32[8,32,2]{1,2,0:T(2,128)}), s32[8,32,2]{1,2,0:T(2,128)S(1)}, u32[]{:S(2)}, u32[]{:S(2)}) async-start(s32[8,32,2]{1,2,0:T(2,128)} %copy.153), calls=%async_computation.1 | async-start | bytes 16384 | tf_op jit(solution)/shard_map/all_to_all | solution.py:109
  72.4 4.6 all-to-all-done.1
  77.3 1.6 pad_maximum_fusion
  78.9 34.8 %while.24 = (s32[]{:T(128)}, f32[8,128,128]{1,2,0:T(8,128)}, s32[8]{0:T(128)S(1)}, f32[1024]{0:T(1024)S(1)}, bf16[768,1024]{1,0:T(8,128)(2,1)S(1)}, /*index=5*/b...) while((s32[]{:T(128)}, f32[8,128,128]{1,2,0:T(8,128)}, ...), condition=%wide.region_4.5_spmd.clone, body=%wide.region_0.4_spmd.sunk.clone | while | flops 137934080 | bytes 1126141 | solution.py:71
  81.5 1.2 conditional.3
  85.8 1.2 conditional.3
  90.2 1.2 conditional.3
  94.5 1.2 conditional.3
  98.9 1.2 conditional.3
  103.2 1.2 conditional.3
  107.6 1.2 conditional.3
  111.9 1.2 conditional.3
  113.8 1.1 fusion.91
  115.0 4.2 collective-permute-start.2
  119.3 10.0 %collective-permute-done.2 = f32[128,512]{1,0:T(8,128)S(1)} collective-permute-done((f32[128,512]{1,0:T(8,128)S(1)}, f32[128,512]{1,0:T(8,128)S(1)}, u32[]{:S(2)}, u32[]{:S(2)}) %collective-permute-start.2) | collective-permute-done | bytes 262176 | tf_op jit(solution)/shard_map/ppermute | solution.py:15
  130.4 18.6 %reshape.238 = f32[1,32,4,8,128]{2,1,4,3,0:T(8,128)} reshape(f32[128,512,2]{0,2,1:T(2,128)S(1)} %copy.146) | data formatting | bytes 1048576 | tf_op jit(solution)/shard_map/reshape | solution.py:132
  149.0 9.2 %copy.147 = f32[1,32,4,8,128]{4,3,0,2,1:T(8,128)} copy(f32[1,32,4,8,128]{2,1,4,3,0:T(8,128)} %reshape.238) | data formatting | bytes 1048576 | tf_op jit(solution)/shard_map/reshape | solution.py:132
  158.3 1.1 add_bitcast_fusion
  159.8 2.0 copy.156
  161.8 6.0 %gather_fusion = f32[512,6,4,128]{3,2,1,0:T(4,128)} fusion(f32[256,6,4,128]{3,2,1,0:T(4,128)S(1)} %copy.156, s32[1024]{0:T(1024)S(1)} %pad_clamp_fusion.1), kind=kCustom, calls=%fused_computation | custom fusion | bytes 12584960 | tf_op jit(solution)/shard_map/gather | solution.py:140
  167.8 4.7 copy.157
  172.5 144.4 %all_to_all.20 = f32[8,32,2,6,4,128]{5,4,3,2,0,1:T(4,128)S(1)} all-to-all(f32[8,32,2,6,4,128]{5,4,3,2,0,1:T(4,128)S(1)} %copy.157), channel_id=1, replica_groups=mesh['lon'=32,'lat'=8] {'lon'}, dimensions={1} | all-to-all | bytes 12582912 | tf_op jit(solution)/shard_map/all_to_all | solution.py:139
  316.9 4.0 copy.158
  320.9 6.7 %all-to-all-start.3 = ((f32[8,32,2,6,4,128]{5,4,3,2,1,0:T(4,128)}), f32[8,32,2,6,4,128]{5,4,3,2,1,0:T(4,128)}, u32[]{:S(2)}, u32[]{:S(2)}) async-start(f32[8,32,2,6,4,128]{5,4,3,2,1,0:T(4,128)} %copy.158), calls=%async_computation.3 | async-start | bytes 12582912 | tf_op jit(solution)/shard_map/all_to_all | solution.py:138
  327.7 1.0 copy.167
  328.7 70.2 %all-to-all-done.3 = f32[8,32,2,6,4,128]{5,4,3,2,1,0:T(4,128)} async-done(((f32[8,32,2,6,4,128]{5,4,3,2,1,0:T(4,128)}), f32[8,32,2,6,4,128]{5,4,3,2,1,0:T(4,128)}, u32[]{:S(2)}, u32[]{:S(2)}) %all-to-all-start.3) | async-done | bytes 6291488 | tf_op jit(solution)/shard_map/all_to_all | solution.py:138
  398.9 5.3 %gather_fusion.1 = f32[256,6,4,128]{3,2,1,0:T(4,128)S(1)} fusion(f32[512,6,4,128]{3,2,1,0:T(4,128)} %bitcast.31, s32[1024]{0:T(1024)S(1)} %pad_clamp_fusion), kind=kCustom, calls=%fused_computation.1 | custom fusion | bytes 6292480 | tf_op jit(solution)/shard_map/gather | solution.py:151
  404.1 77.7 %while.25 = (s32[]{:T(128)}, f32[16,16,6,4,128]{4,1,0,3,2:T(8,128)}, s32[16]{0:T(128)S(1)}, f32[256,6,4,128]{3,2,1,0:T(4,128)S(1)}, s32[256,128]{1,0:T(8,128)}, /*index=5*/f32[256,128]{1,0:T(8,128)}, s32[1]{0:T(128)}) while((s32[]{:T(128)}, f32[16,16,6,4,128]{4,1,0,3,2:T(8,128)}, s32[16]{0:T(128)S(1)}, ...), condition=%wide.region_10.11_spmd.clone, body=%wide.region_9.10_spmd.sunk.clone | while | flops 78432264 | bytes 1327763 | solution.py:166
  406.8 1.5 convolution_bitcast_fusion.3
  408.2 0.8 copy_dynamic-update-slice_fusion.3
  411.6 1.5 convolution_bitcast_fusion.3
  413.1 0.8 copy_dynamic-update-slice_fusion.3
  416.5 1.5 convolution_bitcast_fusion.3
  417.9 0.8 copy_dynamic-update-slice_fusion.3
  421.3 1.5 convolution_bitcast_fusion.3
  422.8 0.8 copy_dynamic-update-slice_fusion.3
  426.2 1.5 convolution_bitcast_fusion.3
  427.6 0.8 copy_dynamic-update-slice_fusion.3
  431.0 1.5 convolution_bitcast_fusion.3
  435.9 1.5 convolution_bitcast_fusion.3
  440.7 1.5 convolution_bitcast_fusion.3
  445.6 1.5 convolution_bitcast_fusion.3
  450.4 1.5 convolution_bitcast_fusion.3
  455.3 1.5 convolution_bitcast_fusion.3
  460.1 1.5 convolution_bitcast_fusion.3
  465.0 1.5 convolution_bitcast_fusion.3
  469.9 1.5 convolution_bitcast_fusion.3
  474.7 1.5 convolution_bitcast_fusion.3
  479.6 1.5 convolution_bitcast_fusion.3
  481.8 2.3 copy.161
  484.1 6.8 %fusion.52 = f32[6,128,8,128]{1,3,0,2:T(8,128)S(1)} fusion(f32[6,128,8,128]{3,2,1,0:T(8,128)S(1)} %bitcast.124, f32[8,128]{1,0:T(8,128)S(1)} %get-tuple-element.353, s32[8,128]{1,0:T(8,128)S(1)} %get-tuple-element.349, f32[8,128]{1,0:T(8,128)S(1)} %get-tuple-element.352, s32[8,128]{1,0:T(8,128)S(1)} %get-tuple-element.348, ...), kind=kOutput, calls=%fused_computation.77 | convolution fusion | flops 1209401344 | bytes 6324224 | tf_op jit(solution)/shard_map/blk,flbc->fkbc/dot_general | solution.py:170
  491.3 5.3 %copy.166 = f32[6,128,1,1024]{3,2,1,0:T(1,128)} copy(f32[6,128,1,1024]{1,3,0,2:T(8,128)S(1)} %bitcast.125) | data formatting | bytes 6291456
  (186 shorter events, 70.4 us)
Async XLA Ops:
  13.6 14.4 %copy-start.7 = (s32[1,256,1]{1,2,0:T(1,128)S(1)}, s32[1,256,1]{1,2,0:T(1,128)}, u32[]{:S(2)}) copy-start(s32[1,256,1]{1,2,0:T(1,128)} %param.26) | copy-start | bytes 3076
  16.7 20.5 %copy-start.10 = (s32[1,1024]{1,0:T(1,128)S(1)}, s32[1,1024]{1,0:T(1,128)}, u32[]{:S(2)}) copy-start(s32[1,1024]{1,0:T(1,128)} %param.20) | copy-start | bytes 12292
  20.1 57.2 %collective-permute-start.1 = (bf16[768,512]{1,0:T(8,128)(2,1)S(1)}, bf16[768,512]{1,0:T(8,128)(2,1)}, u32[]{:S(2)}, u32[]{:S(2)}) collective-permute-start(bf16[768,512]{1,0:T(8,128)(2,1)S(1)} %bitcast.129), channel_id=1, source_target_pairs={{0,128},{8,136},{16,144},{24,152},{32,160},{40,168},{48,176},{56,1... | collective-permute-start | bytes 2359304 | tf_op jit(solution)/shard_map/ppermute | solution.py:15
  31.3 35.2 %all-to-all-start = ((s32[8,32,2]{0,2,1:T(2,128)}), s32[8,32,2]{0,2,1:T(2,128)S(1)}, u32[]{:S(2)}, u32[]{:S(2)}) async-start(s32[8,32,2]{0,2,1:T(2,128)} %copy.152), calls=%async_computation | async-start | bytes 65536 | tf_op jit(solution)/shard_map/all_to_all | solution.py:110
  37.7 34.7 %collective-permute-start = (bf16[512]{0:T(512)(128)(2,1)S(1)}, bf16[512]{0:T(512)(128)(2,1)S(1)}, u32[]{:S(2)}, u32[]{:S(2)}) collective-permute-start(bf16[512]{0:T(512)(128)(2,1)S(1)} %get-tuple-element.299), channel_id=1, source_target_pairs={{0,128},{8,136},{16,144},{24,152},{32,160},{40,168},{48,176},{56,1... | collective-permute-start | bytes 3080 | tf_op jit(solution)/shard_map/ppermute | solution.py:15
  43.0 3.3 copy-start.3
  43.0 3.4 copy-start.4
  43.0 35.9 %copy-start.2 = (bf16[64,768]{1,0:T(8,128)(2,1)S(1)}, bf16[64,768]{1,0:T(8,128)(2,1)}, u32[]{:S(2)}) copy-start(bf16[64,768]{1,0:T(8,128)(2,1)} %param.21) | copy-start | bytes 294916
  43.0 35.9 %copy-start.5 = (f32[224]{0:T(256)S(1)}, f32[224]{0:T(256)}, u32[]{:S(2)}) copy-start(f32[224]{0:T(256)} %param.24) | copy-start | bytes 2692
  43.0 35.9 %copy-start.6 = (f32[64]{0:T(128)S(1)}, f32[64]{0:T(128)}, u32[]{:S(2)}) copy-start(f32[64]{0:T(128)} %param.22) | copy-start | bytes 772
  67.2 9.9 %all-to-all-start.1 = ((s32[8,32,2]{1,2,0:T(2,128)}), s32[8,32,2]{1,2,0:T(2,128)S(1)}, u32[]{:S(2)}, u32[]{:S(2)}) async-start(s32[8,32,2]{1,2,0:T(2,128)} %copy.153), calls=%async_computation.1 | async-start | bytes 16384 | tf_op jit(solution)/shard_map/all_to_all | solution.py:109
  115.0 14.4 %collective-permute-start.2 = (f32[128,512]{1,0:T(8,128)S(1)}, f32[128,512]{1,0:T(8,128)S(1)}, u32[]{:S(2)}, u32[]{:S(2)}) collective-permute-start(f32[128,512]{1,0:T(8,128)S(1)} %copy.177), channel_id=1, source_target_pairs={{0,128},{8,136},{16,144},{24,152},{32,160},{40,168},{48,176},{56,1... | collective-permute-start | bytes 786440 | tf_op jit(solution)/shard_map/ppermute | solution.py:15
  129.6 0.8 copy-start
  149.0 9.2 %slice-start = ((f32[6,128,1,1024]{3,2,1,0:T(1,128)}), f32[1,128,1,1024]{3,2,1,0:T(1,128)S(1)}, s32[]{:S(2)}) async-start(f32[6,128,1,1024]{3,2,1,0:T(1,128)} %param.19), calls=%async_computation.4 | async-start | bytes 1048576 | tf_op jit(solution)/shard_map/slice | solution.py:133
  149.0 10.4 %slice-start.1 = ((f32[6,128,1,1024]{3,2,1,0:T(1,128)}), f32[5,128,1,1024]{3,2,1,0:T(1,128)S(1)}, s32[]{:S(2)}) async-start(f32[6,128,1,1024]{3,2,1,0:T(1,128)} %param.19), calls=%async_computation.5 | async-start | bytes 5242880 | tf_op jit(solution)/shard_map/slice | solution.py:134
  320.9 6.7 %copy-start.8 = (s32[1,8,128]{2,1,0:T(8,128)S(1)}, s32[1,8,128]{2,1,0:T(8,128)}, u32[]{:S(2)}) copy-start(s32[1,8,128]{2,1,0:T(8,128)} %param.31) | copy-start | bytes 12292
  320.9 6.8 %copy-start.9 = (f32[1,8,128]{2,1,0:T(8,128)S(1)}, f32[1,8,128]{2,1,0:T(8,128)}, u32[]{:S(2)}) copy-start(f32[1,8,128]{2,1,0:T(8,128)} %param.30) | copy-start | bytes 12292
  320.9 6.8 %copy-start.1 = (f32[128,512,2]{0,2,1:T(2,128)S(1)}, f32[128,512,2]{0,2,1:T(2,128)}, u32[]{:S(2)}) copy-start(f32[128,512,2]{0,2,1:T(2,128)} %copy-done) | copy-start | bytes 1572868
  320.9 78.0 %all-to-all-start.3 = ((f32[8,32,2,6,4,128]{5,4,3,2,1,0:T(4,128)}), f32[8,32,2,6,4,128]{5,4,3,2,1,0:T(4,128)}, u32[]{:S(2)}, u32[]{:S(2)}) async-start(f32[8,32,2,6,4,128]{5,4,3,2,1,0:T(4,128)} %copy.158), calls=%async_computation.3 | async-start | bytes 12582912 | tf_op jit(solution)/shard_map/all_to_all | solution.py:138
where the time goes:
time: 499 us; the launch traced here: 497 us
  blocking collectives  144 us (29%)
  local copies, waits for them, and re-layouts  116 us (23%)
  waiting for transfers between devices  105 us (21%)
  matrix products  39.4 us (8%)
  other arithmetic  36.1 us (7%)
  starting transfers between devices  35.1 us (7%)
  loops' own time  19.4 us (4%)
    all_to_all x1, blocking collectives, per_device(): lax.all_to_all(unit_data[picked].reshape(lat_n, lon_n, slot_count, unit_d...  144 us
    all_to_all x1, waiting for transfers between devices, per_device(): lax.all_to_all(lax.all_to_all(unit_data[picked].reshape(lat_n, lon_n, slo...  70.2 us
    reshape x2, local copies, waits for them, and re-layouts, per_device(): jnp.stack([mixed_heat[:, :half_cols], returned], axis=-1)  27.8 us
    dot_general x16, matrix products, trace_group(): jnp.einsum('ufgr,urc->ufgc', source_rows, matrix, precision=lax.Precision...  23.3 us
    all_to_all x1, waiting for transfers between devices, per_device(): lax.all_to_all(wanted.reshape(lat_n, lon_n, slot_count), 'lon', split_axi...  20 us
    ppermute x3, starting transfers between devices, from_partner(): return lax.ppermute(value, axis, pairs)  17.2 us
    dynamic_update_slice x16, local copies, waits for them, and re-layouts, per_device(): lax.map(trace_group, jnp.arange(units_n // group_size, dtype=jnp.int32))  12.8 us
    div x17, other arithmetic, cubic_weights(): -fraction * (fraction - 1.0) * (fraction - 2.0) / 6.0  11.4 us
  transfers between devices with their start and end apart: 6, of which 4 were waited for; matrix products, arithmetic and copies ran while one was open for 2% of the time, Pallas kernels for 0%

commit v1 on v0

v1 whole, which is shorter than its diff:
```python
import functools

import jax
import jax.numpy as jnp
from jax import lax
from jax.experimental import pallas as pl
from jax.experimental.pallas import tpu as pltpu
from jax.sharding import PartitionSpec as P

BLOCK = 128
LG = 4
PAIRS = 3
UNROLL = 16
VERTICAL_UNROLL = 8
PACK_STEPS = 2
AXES = ("lat", "lon")
CODE = 16480.0
SPLIT = 2.0**-75
DECODE = float((65536.0 * CODE) ** -5 / SPLIT)


def cubic_weights(fraction, scale=1.0):
    return (
        -fraction * (fraction - 1.0) * (fraction - 2.0) * (scale / 6.0),
        (fraction + 1.0) * (fraction - 1.0) * (fraction - 2.0) * (scale / 2.0),
        -(fraction + 1.0) * fraction * (fraction - 2.0) * (scale / 2.0),
        (fraction + 1.0) * fraction * (fraction - 1.0) * (scale / 6.0),
    )


def halves(value):
    high = value.astype(jnp.bfloat16)
    return high, (value - high.astype(jnp.float32)).astype(jnp.bfloat16)


def mxu(a, b, a_dim):
    return lax.dot_general(a, b, (((a_dim,), (0,)), ((), ())), preferred_element_type=jnp.float32)


def softplus(v):
    u = jnp.exp(-jnp.abs(v))
    return jnp.maximum(v, 0.0) + jnp.where(
        u < 0.01, u * (1.0 - u * (0.5 - u * (1.0 / 3.0 - u * 0.25))), jnp.log(1.0 + u)
    )


def coded(x):
    root = jnp.exp2(jnp.log2(jnp.abs(x)) * 0.2) * CODE
    return jnp.where(x < 0.0, -root, root)


def nearest(value):
    return jnp.floor(value + 0.5).astype(jnp.int32)


def word_of(first, second):
    low = nearest(coded(second)) & 0xFFFF
    high = nearest(coded(first) - low.astype(jnp.float32) * (1.0 / 65536.0))
    return (high << 16) | low


def heat_kernel(x, sun, w_in, b_in, w_out, b_out, level_map, heat, code):
    outs, levels = level_map.shape
    hid, feats = w_in.shape
    blocks = sun.shape[0]
    width = 2 * BLOCK
    bias_in = jnp.broadcast_to(b_in[...], (width, hid)).T
    bias_out = jnp.broadcast_to(b_out[...], (width, outs)).T
    lower = (
        lax.broadcasted_iota(jnp.int32, (outs, outs), 0)
        >= lax.broadcasted_iota(jnp.int32, (outs, outs), 1)
    ).astype(jnp.float32).astype(jnp.bfloat16)
    map_high, map_low = halves(level_map[...])

    def two_blocks(step, carry):
        b = step * 2
        features = jnp.concatenate(
            [x[pl.ds(b + i, feats, stride=blocks), :] for i in range(2)], axis=1
        ).astype(jnp.bfloat16)
        hidden = jnp.tanh(mxu(w_in[...], features, 1) + bias_in).astype(jnp.bfloat16)
        optical = softplus(mxu(w_out[...], hidden, 0) + bias_out) * (4.0 / outs)
        high, rest = halves(optical)
        middle = (optical - high.astype(jnp.float32)) - rest.astype(jnp.float32)
        depth = mxu(lower, high, 1) + mxu(lower, rest, 1) + mxu(lower, middle.astype(jnp.bfloat16), 1)
        high, rest = halves(optical * jnp.exp(-depth))
        warm = mxu(map_high, high, 0) + mxu(map_high, rest, 0) + mxu(map_low, high, 0)
        for i in range(2):
            lit = sun[pl.ds(b + i, 1), :].astype(jnp.float32)
            heat[pl.ds(b + i, levels, stride=blocks), :] = warm[:, i * BLOCK : (i + 1) * BLOCK] * lit
        return carry

    lax.fori_loop(0, blocks // 2, two_blocks, 0)
    rows = levels * blocks
    chunk = 64

    def code_rows(step, carry):
        at = pl.multiple_of(step * chunk, chunk)
        here = pl.ds(at, chunk)
        for p in range(PAIRS):
            first = x[pl.ds(at + p * rows, chunk), :]
            if p == 0:
                first = first + heat[here, :]
            second = x[pl.ds(at + (p + PAIRS) * rows, chunk), :]
            code[pl.ds(at + p * rows, chunk), :] = word_of(first, second)
        return carry

    lax.fori_loop(0, rows // chunk, code_rows, 0)


def ask_kernel(owner, unit, asked):
    devices = asked.shape[0]
    units = owner.shape[1]
    blocks = 8
    rows = units * LG
    start = (unit[...] // blocks) * (LG * blocks) + unit[...] % blocks
    key = (lax.broadcasted_iota(jnp.int32, (1, units), 1) * rows + start).astype(jnp.float32)
    named = owner[...] == lax.broadcasted_iota(jnp.int32, (devices, units), 0)
    low = jnp.min(jnp.where(named, key, float(units * rows)), axis=1, keepdims=True)
    high = jnp.max(jnp.where(named, key, 0.0), axis=1, keepdims=True)
    low = low.astype(jnp.int32) & (rows - 1)
    high = high.astype(jnp.int32) & (rows - 1)
    asked[...] = jnp.broadcast_to(low | (high << 16), asked.shape)


def pack_kernel(asked, code, sent, row, starts, sem):
    devices = sent.shape[0]
    rows = code.shape[0] // PAIRS

    @pl.when(pl.program_id(0) == 0)
    def _():
        diagonal = lax.broadcasted_iota(jnp.int32, (BLOCK, BLOCK), 0) == lax.broadcasted_iota(
            jnp.int32, (BLOCK, BLOCK), 1
        )
        for i in range(asked.shape[0] // BLOCK):
            tile = jnp.where(diagonal, asked[pl.ds(i * BLOCK, BLOCK), :], 0)
            row[pl.ds(i, 1), :] = jnp.sum(tile, axis=0, keepdims=True)
        copy = pltpu.make_async_copy(row, starts, sem)
        copy.start()
        copy.wait()

    base = pl.program_id(0) * devices

    def one(d, carry):
        owner = base + d
        both = starts[owner >> 7, owner & (BLOCK - 1)]
        for j, at in enumerate((both & 0xFFFF, both >> 16)):
            for p in range(PAIRS):
                sent[d, pl.ds((j * PAIRS + p) * LG, LG), :] = code[
                    pl.ds(at + p * rows, LG, stride=8), :
                ]
        return carry

    lax.fori_loop(0, devices, one, 0, unroll=16)


def prepare_kernel(h_frac, h_shift, v_frac, v_shift, weights, places, v_high, v_low):
    units = h_frac.shape[0]
    blocks, levels = v_frac.shape
    lane = lax.broadcasted_iota(jnp.int32, (units, BLOCK), 1)
    for k, weight in enumerate(cubic_weights(h_frac[...])):
        weights[pl.ds(k * units, units), :] = weight * DECODE
        places[pl.ds(k * units, units), :] = jnp.clip(lane + h_shift[...] + (k - 1), 0, BLOCK - 1)
    source = lax.broadcasted_iota(jnp.int32, (levels, levels), 0)
    target = lax.broadcasted_iota(jnp.int32, (1, levels), 1)

    def one_block(b, carry):
        vertical = jnp.zeros((levels, levels), jnp.float32)
        shift = v_shift[pl.ds(b, 1), :]
        for j, weight in enumerate(cubic_weights(v_frac[pl.ds(b, 1), :])):
            at = jnp.clip(target + shift + (j - 1), 0, levels - 1)
            vertical = vertical + jnp.where(source == at, weight * SPLIT, 0.0)
        high, low = halves(vertical.T)
        here = pl.ds(pl.multiple_of(b * levels, levels), levels)
        v_high[here, :] = high
        v_low[here, :] = low
        return carry

    lax.fori_loop(0, blocks, one_block, 0)


def lanes_at(value, index):
    numbers = lax.GatherDimensionNumbers(
        offset_dims=(),
        collapsed_slice_dims=(1,),
        start_index_map=(1,),
        operand_batching_dims=(0,),
        start_indices_batching_dims=(0,),
    )
    return lax.gather(
        value, index[..., None], numbers, (1, 1), mode=lax.GatherScatterMode.PROMISE_IN_BOUNDS
    )


def fifth_times(word, weight):
    y = word.astype(jnp.float32)
    square = y * y
    return (y * weight) * square * square


def advect_kernel(landing, got, weights, places, v_high, v_low, out, traced, moved_all, sems):
    units = places.shape[0] // 4
    levels = v_high.shape[1]
    blocks = v_high.shape[0] // levels
    groups = levels // LG
    rows = levels * blocks
    fields = 2 * PAIRS
    upper = lax.broadcasted_iota(jnp.int32, (2 * LG, BLOCK), 0) < LG

    def one_block(b, carry):
        base = b * (fields * levels)

        def two_units(step, inner):
            unit = [(step * 2 + i) * blocks + b for i in range(2)]
            row = [landing[u] * (PAIRS * LG) for u in unit]
            tails = [got[pl.ds(r + LG, 2 * LG), :] for r in row]
            words = [got[pl.ds(r, 2 * LG), :] for r in row]
            words.append(jnp.where(upper, pltpu.roll(tails[0], LG, 0), tails[1]))
            sums = [None] * 6
            for k in range(4):
                index = [places[pl.ds(u + k * units, 2 * LG, stride=0), :] for u in unit]
                weight = [weights[pl.ds(u + k * units, 2 * LG, stride=0), :] for u in unit]
                index.append(jnp.where(upper, index[0], index[1]))
                weight.append(jnp.where(upper, weight[0], weight[1]))
                for n in range(3):
                    word = lanes_at(words[n], index[n])
                    for half, part in enumerate((word, word << 16)):
                        term = fifth_times(part, weight[n])
                        at = n * 2 + half
                        sums[at] = term if k == 0 else sums[at] + term
            for n in range(2):
                for half in range(2):
                    for i in range(2):
                        f = i + half * PAIRS
                        traced[pl.ds(base + f * levels + (step * 2 + n) * LG, LG), :] = sums[n * 2 + half][
                            i * LG : (i + 1) * LG
                        ]
            for half in range(2):
                f = 2 + half * PAIRS
                at = pl.multiple_of(base + f * levels + step * 2 * LG, 2 * LG)
                traced[pl.ds(at, 2 * LG), :] = sums[4 + half]
            return inner

        lax.fori_loop(0, groups // 2, two_units, 0, unroll=UNROLL)
        return carry

    lax.fori_loop(0, blocks, one_block, 0)
    copies = []
    for first in range(0, fields, 2):

        def one_vertical(b, carry):
            at = pl.multiple_of(b * (fields * levels), levels)
            wide = jnp.concatenate(
                [traced[pl.ds(at + (first + i) * levels, levels), :] for i in range(2)], axis=1
            )
            t_high, t_low = halves(wide)
            here = pl.ds(pl.multiple_of(b * levels, levels), levels)
            high, low = v_high[here, :], v_low[here, :]
            moved = mxu(
                jnp.concatenate([high, high], axis=1), jnp.concatenate([t_high, t_low], axis=0), 1
            ) + mxu(low, t_high, 1)
            for i in range(2):
                moved_all[pl.ds((first + i) * rows + b, levels, stride=blocks), :] = moved[
                    :, i * BLOCK : (i + 1) * BLOCK
                ]
            return carry

        lax.fori_loop(0, blocks, one_vertical, 0, unroll=VERTICAL_UNROLL)
        here = pl.ds(first * rows, 2 * rows)
        copies.append(pltpu.make_async_copy(moved_all.at[here, :], out.at[here, :], sems.at[first // 2]))
        copies[-1].start()
    for copy in copies:
        copy.wait()


VMEM = pl.BlockSpec(memory_space=pltpu.VMEM)
SMEM = pl.BlockSpec(memory_space=pltpu.SMEM)
ANY = pl.BlockSpec(memory_space=pl.ANY)


def keep_near(value):
    return pltpu.with_memory_space_constraint(value, pltpu.VMEM)


def exchange(value):
    return lax.all_to_all(value, AXES, split_axis=0, concat_axis=0, tiled=True)


def heat(fields, sunlit, w_in, b_in, w_out, b_out, level_map):
    n_fields, levels, _, columns = fields.shape
    blocks = columns // BLOCK
    rows = levels * blocks
    return pl.pallas_call(
        heat_kernel,
        out_shape=(
            jax.ShapeDtypeStruct((rows, BLOCK), jnp.float32),
            jax.ShapeDtypeStruct((PAIRS * rows, BLOCK), jnp.int32),
        ),
        in_specs=[VMEM] * 7,
        out_specs=(VMEM, VMEM),
        compiler_params=pltpu.CompilerParams(vmem_limit_bytes=20 << 20),
        name="heat",
    )(
        fields.reshape(n_fields * rows, BLOCK),
        sunlit.reshape(blocks, BLOCK),
        w_in,
        b_in.reshape(1, -1),
        w_out.T,
        b_out.reshape(1, -1),
        level_map.T,
    )


def ask(owner, unit, devices):
    return pl.pallas_call(
        ask_kernel,
        out_shape=jax.ShapeDtypeStruct((devices, BLOCK), jnp.int32),
        in_specs=[VMEM] * 2,
        out_specs=VMEM,
        compiler_params=pltpu.CompilerParams(vmem_limit_bytes=8 << 20),
        name="ask",
    )(owner, unit)


def pack(asked, code):
    devices = asked.shape[0]
    shape = (devices, 2 * PAIRS * LG, BLOCK)
    return pl.pallas_call(
        pack_kernel,
        grid=(PACK_STEPS,),
        out_shape=jax.ShapeDtypeStruct(shape, jnp.int32),
        in_specs=[VMEM] * 2,
        out_specs=pl.BlockSpec((devices // PACK_STEPS,) + shape[1:], lambda i: (i, 0, 0)),
        scratch_shapes=[
            pltpu.VMEM((devices // BLOCK, BLOCK), jnp.int32),
            pltpu.SMEM((devices // BLOCK, BLOCK), jnp.int32),
            pltpu.SemaphoreType.DMA,
        ],
        compiler_params=pltpu.CompilerParams(vmem_limit_bytes=12 << 20),
        name="pack",
    )(keep_near(asked), keep_near(code))


def prepare(h_frac, h_shift, v_frac, v_shift):
    units = h_frac.shape[0]
    blocks, levels = v_frac.shape
    return pl.pallas_call(
        prepare_kernel,
        out_shape=(
            jax.ShapeDtypeStruct((4 * units, BLOCK), jnp.float32),
            jax.ShapeDtypeStruct((4 * units, BLOCK), jnp.int32),
            jax.ShapeDtypeStruct((blocks * levels, levels), jnp.bfloat16),
            jax.ShapeDtypeStruct((blocks * levels, levels), jnp.bfloat16),
        ),
        in_specs=[VMEM] * 4,
        out_specs=(VMEM,) * 4,
        compiler_params=pltpu.CompilerParams(vmem_limit_bytes=12 << 20),
        name="prepare",
    )(h_frac, h_shift, v_frac, v_shift)


def advect(landing, got, prepared):
    levels = prepared[2].shape[1]
    rows = prepared[2].shape[0]
    fields = 2 * PAIRS
    return pl.pallas_call(
        advect_kernel,
        out_shape=jax.ShapeDtypeStruct((fields * rows, BLOCK), jnp.float32),
        in_specs=[SMEM] + [VMEM] * 5,
        out_specs=ANY,
        scratch_shapes=[
            pltpu.VMEM((fields * rows, BLOCK), jnp.float32),
            pltpu.VMEM((fields * rows, BLOCK), jnp.float32),
            pltpu.SemaphoreType.DMA((PAIRS,)),
        ],
        compiler_params=pltpu.CompilerParams(vmem_limit_bytes=24 << 20),
        name="advect",
    )(landing, keep_near(got.reshape(-1, BLOCK)), *[keep_near(p) for p in prepared])


def per_device(
    fields,
    sunlit,
    w_in,
    b_in,
    w_out,
    b_out,
    level_map,
    dep_owner,
    owner_unit,
    h_frac,
    h_shift,
    v_frac,
    v_shift,
):
    n_fields, levels, _, columns = fields.shape
    units = owner_unit.shape[1]
    devices = lax.axis_size("lat") * lax.axis_size("lon")
    owners = dep_owner[0, :, 0]
    order = jnp.arange(units, dtype=jnp.int32)
    asked = exchange(ask(owners.reshape(1, units), owner_unit, devices)[:, None, :])
    second = jnp.any((owners[:, None] == owners[None, :]) & (order[:, None] > order[None, :]), axis=1)
    landing = owners * 2 + second.astype(jnp.int32)
    heating, code = heat(fields, sunlit, w_in, b_in, w_out, b_out, level_map)
    got = exchange(pack(asked.reshape(devices, BLOCK), code))
    prepared = prepare(h_frac[0], h_shift[0], v_frac[0], v_shift[0])
    advected = advect(landing, got, prepared)
    return (advected.reshape(n_fields, levels, 1, columns), heating.reshape(levels, 1, columns))


def solution(mesh):
    placed = (
        P(None, None, "lat", "lon"),
        P("lat", "lon"),
        P(),
        P(),
        P(),
        P(),
        P(),
        P("lat", "lon", None),
        P("lat", "lon"),
        P("lat", "lon", None),
        P("lat", "lon", None),
        P("lat", "lon", None),
        P("lat", "lon", None),
    )
    return jax.shard_map(
        per_device,
        mesh=mesh,
        in_specs=placed,
        out_specs=(P(None, None, "lat", "lon"), P(None, "lat", "lon")),
        check_vma=False,
    )
```

time: 499 us -> 136 us (0.27)
  blocking collectives: 144 us -> 0 us
  local copies, waits for them, and re-layouts: 116 us -> 14 us
  matrix products: 39.4 us -> 0 us
  other arithmetic: 36.1 us -> 0.19 us
  waiting for transfers between devices: 105 us -> 71.5 us
  Pallas kernels: 0 us -> 19.5 us
  loops' own time: 19.4 us -> 0 us
  starting transfers between devices: 35.1 us -> 29.4 us
    all_to_all x1 -> x0, blocking collectives: 144 us -> none  [per_device(): lax.all_to_all(unit_data[picked].reshape(lat_n, lon_n, slot_count, unit_d...]
    dot_general x41 -> x0, matrix products: 39.4 us -> none  [the longest x16 23.3 us: trace_group(): jnp.einsum('ufgr,urc->ufgc', source_rows, matrix, precision=lax.Precision...]
    reshape x6 -> x0, local copies, waits for them, and re-layouts: 35.5 us -> none  [the longest x2 27.8 us: per_device(): jnp.stack([mixed_heat[:, :half_cols], returned], axis=-1)]
    all_to_all x3 -> x2, waiting for transfers between devices: 94.8 us -> 71.5 us  [exchange(): return lax.all_to_all(value, AXES, split_axis=0, concat_axis=0, tiled=True)]
    pallas_call x0 -> x5, Pallas kernels: none -> 19.5 us  [the longest x1 7.61 us: advect(): pl.pallas_call(advect_kernel, out_shape=jax.ShapeDtypeStruct((fields * ro...]
    another operation x10 -> x0, loops' own time: 19.4 us -> none  [the longest x1 9.85 us: heat_all(): stacked = lax.map(one_block, jnp.arange(blocks_n, dtype=jnp.int32))]
    dynamic_update_slice x24 -> x0, local copies, waits for them, and re-layouts: 17.9 us -> none  [the longest x16 12.8 us: per_device(): lax.map(trace_group, jnp.arange(units_n // group_size, dtype=jnp.int32))]
    ppermute x3 -> x0, starting transfers between devices: 17.2 us -> none  [from_partner(): return lax.ppermute(value, axis, pairs)]
  transfers between devices with their start and end apart: 6 -> 2, of which waited for: 4 -> 1; matrix products, arithmetic and copies ran while one was open for 2% -> 0% of each run, Pallas kernels for 0% -> 6%
where the time goes in v1:
time: 136 us; the launch traced here: 135 us
  waiting for transfers between devices  71.5 us (53%)
  starting transfers between devices  29.4 us (22%)
  Pallas kernels  19.5 us (14%)
  local copies, waits for them, and re-layouts  14 us (10%)
    all_to_all x2, waiting for transfers between devices, exchange(): return lax.all_to_all(value, AXES, split_axis=0, concat_axis=0, tiled=True)  71.5 us
    all_to_all x2, starting transfers between devices, exchange(): return lax.all_to_all(value, AXES, split_axis=0, concat_axis=0, tiled=True)  29.4 us
    unnamed x40, local copies, waits for them, and re-layouts  14 us
    pallas_call x1, Pallas kernels, advect(): pl.pallas_call(advect_kernel, out_shape=jax.ShapeDtypeStruct((fields * ro...  7.61 us
    pallas_call x1, Pallas kernels, heat(): pl.pallas_call(heat_kernel, out_shape=(jax.ShapeDtypeStruct((rows, BLOCK)...  7.02 us
    pallas_call x1, Pallas kernels, pack(): pl.pallas_call(pack_kernel, grid=(PACK_STEPS,), out_shape=jax.ShapeDtypeS...  2.93 us
  transfers between devices with their start and end apart: 2, of which 1 were waited for; matrix products, arithmetic and copies ran while one was open for 0% of the time, Pallas kernels for 6%

profile of v1, /device:TPU:1, one launch (start us, length us, event | category | flops | bytes accessed | tf_op | source)
XLA Modules:
  0.0 135.4 jit_solution(15505343138559912299)
XLA Ops:
  0.6 0.0 copy-start.12
  0.6 0.7 copy-done.12
  1.3 0.0 copy-start.17
  1.3 0.7 copy-done.17
  2.0 0.8 ask.1
  2.8 15.6 %all-to-all-start = ((s32[256,1,128]{2,1,0:T(1,128)}), s32[256,1,128]{2,1,0:T(1,128)S(1)}, u32[]{:S(2)}, u32[]{:S(2)}) async-start(s32[256,1,128]{2,1,0:T(1,128)} %bitcast.3), calls=%async_computation | async-start | bytes 262144 | tf_op jit(solution)/shard_map/all_to_all | solution.py:285
  18.5 0.0 copy-start
  18.5 1.9 %copy-done = f32[6,128,1,1024]{3,2,1,0:T(1,128)S(1)} copy-done((f32[6,128,1,1024]{3,2,1,0:T(1,128)S(1)}, f32[6,128,1,1024]{3,2,1,0:T(1,128)}, u32[]{:S(2)}) %copy-start) | copy-done | bytes 3145752
  20.4 0.0 copy-start.9
  20.4 0.9 copy-done.9
  21.3 0.0 copy-start.10
  21.3 0.9 copy-done.10
  22.2 0.0 copy-start.11
  22.2 0.8 copy-done.11
  22.9 0.0 copy-start.14
  22.9 0.7 copy-done.14
  23.6 0.0 copy-start.18
  23.6 0.7 copy-done.18
  24.3 0.0 copy-start.19
  24.3 0.7 copy-done.19
  24.9 7.0 %heat.1 = (f32[1024,128]{1,0:T(8,128)}, s32[3072,128]{1,0:T(8,128)S(1)}) custom-call(f32[6144,128]{1,0:T(8,128)S(1)} %bitcast.20, s32[8,128]{1,0:T(8,128)S(1)} %bitcast.29, bf16[64,768]{1,0:T(8,128)(2,1)S(1)} %copy-done.10, f32[1,64]{1,0:T(1,128)S(1)} %bitcast.33, bf16[64,224]{1,0:T(8,128)(2,1)S(1)} %bitcast.25, f32[1,224]{1,0:T(1,128)S(1)} %bitcast.32, ...), custom_call_target="tpu_custom_call" | custom-call | tf_op jit(solution)/shard_map/heat/pallas_call | solution.py:292
  32.0 0.0 all-to-all-done
  32.0 2.9 %pack.1 = s32[256,24,128]{2,1,0:T(8,128)} custom-call(s32[256,128]{1,0:T(8,128)S(1)} %bitcast.21, s32[3072,128]{1,0:T(8,128)S(1)} %get-tuple-element.8.code), custom_call_target="tpu_custom_call" | custom-call | tf_op jit(solution)/shard_map/pack/pallas_call | solution.py:327
  34.9 0.0 copy-start.7
  34.9 0.0 copy-start.15
  34.9 0.0 copy-start.16
  34.9 0.0 copy-start.13
  35.0 13.7 %all-to-all-start.1 = ((s32[256,24,128]{2,1,0:T(8,128)}), s32[256,24,128]{2,1,0:T(8,128)S(1)}, u32[]{:S(2)}, u32[]{:S(2)}) async-start(s32[256,24,128]{2,1,0:T(8,128)} %pack.1), calls=%async_computation.1 | async-start | bytes 6291456 | tf_op jit(solution)/shard_map/all_to_all | solution.py:285
  48.7 0.0 copy-done.7
  48.7 0.0 copy-done.15
  48.7 0.0 copy-done.16
  48.7 0.0 copy-start.8
  48.7 0.9 copy-done.8
  49.6 1.1 prepare.1
  50.8 0.0 copy-start.1
  50.8 0.8 copy-done.1
  51.6 0.0 copy-start.3
  51.6 0.8 copy-done.3
  52.4 0.0 copy-start.5
  52.4 0.7 copy-done.5
  53.1 0.0 copy-done.13
  53.1 0.2 fusion.1
  53.2 71.5 %all-to-all-done.1 = s32[256,24,128]{2,1,0:T(8,128)S(1)} async-done(((s32[256,24,128]{2,1,0:T(8,128)}), s32[256,24,128]{2,1,0:T(8,128)S(1)}, u32[]{:S(2)}, u32[]{:S(2)}) %all-to-all-start.1) | async-done | bytes 3145760 | tf_op jit(solution)/shard_map/all_to_all | solution.py:285
  124.8 0.0 copy-start.2
  124.8 1.0 copy-done.2
  125.8 0.0 copy-start.4
  125.8 1.0 copy-done.4
  126.9 0.0 copy-start.6
  126.9 0.9 copy-done.6
  127.8 7.6 %advect.1 = f32[6144,128]{1,0:T(8,128)} custom-call(s32[256]{0:T(256)S(1)} %convert_add_fusion.landing, s32[6144,128]{1,0:T(8,128)S(1)} %bitcast.19, f32[1024,128]{1,0:T(8,128)S(1)} %copy-done.2, s32[1024,128]{1,0:T(8,128)S(1)} %copy-done.4, bf16[1024,128]{1,0:T(8,128)(2,1)S(1)} %get-tuple-element.11.v_high, bf16[1024,128]{1,0:T(8,128)(2,1)S(1)} %copy-done.6), custom_call_target="tpu_custom_call" | custom-call | tf_op jit(solution)/shard_map/advect/pallas_call | solution.py:365
  (1 shorter events, 0.0 us)
Async XLA Ops:
  0.6 0.7 copy-start.12
  1.3 0.7 copy-start.17
  2.8 29.1 %all-to-all-start = ((s32[256,1,128]{2,1,0:T(1,128)}), s32[256,1,128]{2,1,0:T(1,128)S(1)}, u32[]{:S(2)}, u32[]{:S(2)}) async-start(s32[256,1,128]{2,1,0:T(1,128)} %bitcast.3), calls=%async_computation | async-start | bytes 262144 | tf_op jit(solution)/shard_map/all_to_all | solution.py:285
  18.5 1.9 %copy-start = (f32[6,128,1,1024]{3,2,1,0:T(1,128)S(1)}, f32[6,128,1,1024]{3,2,1,0:T(1,128)}, u32[]{:S(2)}) copy-start(f32[6,128,1,1024]{3,2,1,0:T(1,128)} %param.13) | copy-start | bytes 9437188
  20.4 0.9 copy-start.9
  21.3 0.9 copy-start.10
  22.2 0.8 copy-start.11
  22.9 0.7 copy-start.14
  23.6 0.7 copy-start.18
  24.3 0.7 copy-start.19
  34.9 13.8 %copy-start.7 = (f32[1,256,128]{2,1,0:T(8,128)S(1)}, f32[1,256,128]{2,1,0:T(8,128)}, u32[]{:S(2)}) copy-start(f32[1,256,128]{2,1,0:T(8,128)} %param.22) | copy-start | bytes 393220
  34.9 13.8 %copy-start.15 = (f32[1,8,128]{2,1,0:T(8,128)S(1)}, f32[1,8,128]{2,1,0:T(8,128)}, u32[]{:S(2)}) copy-start(f32[1,8,128]{2,1,0:T(8,128)} %param.24) | copy-start | bytes 12292
  34.9 13.8 %copy-start.16 = (s32[1,8,128]{2,1,0:T(8,128)S(1)}, s32[1,8,128]{2,1,0:T(8,128)}, u32[]{:S(2)}) copy-start(s32[1,8,128]{2,1,0:T(8,128)} %param.25) | copy-start | bytes 12292
  34.9 18.1 %copy-start.13 = (s32[1,256,1]{1,2,0:T(1,128)S(1)}, s32[1,256,1]{1,2,0:T(1,128)}, u32[]{:S(2)}) copy-start(s32[1,256,1]{1,2,0:T(1,128)} %param.20) | copy-start | bytes 3076
  35.0 89.8 %all-to-all-start.1 = ((s32[256,24,128]{2,1,0:T(8,128)}), s32[256,24,128]{2,1,0:T(8,128)S(1)}, u32[]{:S(2)}, u32[]{:S(2)}) async-start(s32[256,24,128]{2,1,0:T(8,128)} %pack.1), calls=%async_computation.1 | async-start | bytes 6291456 | tf_op jit(solution)/shard_map/all_to_all | solution.py:285
  48.7 0.9 copy-start.8
  50.8 0.8 copy-start.1
  51.6 0.8 copy-start.3
  52.4 0.7 copy-start.5
  124.8 1.0 copy-start.2
  125.8 1.0 copy-start.4
  126.9 0.9 copy-start.6

commit v2 on v1

--- a/solution.py
+++ b/solution.py
@@ -12,7 +12,7 @@
 PAIRS = 3
 UNROLL = 16
 VERTICAL_UNROLL = 8
-PACK_STEPS = 2
+PACK_STEPS = 8
 AXES = ("lat", "lon")
 CODE = 16480.0
 SPLIT = 2.0**-75
@@ -300,14 +300,23 @@
         compiler_params=pltpu.CompilerParams(vmem_limit_bytes=20 << 20),
         name="heat",
     )(
-        fields.reshape(n_fields * rows, BLOCK),
-        sunlit.reshape(blocks, BLOCK),
-        w_in,
-        b_in.reshape(1, -1),
-        w_out.T,
-        b_out.reshape(1, -1),
-        level_map.T,
-    )
+        *map(
+            keep_far,
+            (
+                fields.reshape(n_fields * rows, BLOCK),
+                sunlit.reshape(blocks, BLOCK),
+                w_in,
+                b_in.reshape(1, -1),
+                w_out.T,
+                b_out.reshape(1, -1),
+                level_map.T,
+            ),
+        )
+    )
+
+
+def keep_far(value):
+    return pltpu.with_memory_space_constraint(value, pltpu.HBM)
 
 
 def ask(owner, unit, devices):
@@ -316,7 +325,6 @@
         out_shape=jax.ShapeDtypeStruct((devices, BLOCK), jnp.int32),
         in_specs=[VMEM] * 2,
         out_specs=VMEM,
-        compiler_params=pltpu.CompilerParams(vmem_limit_bytes=8 << 20),
         name="ask",
     )(owner, unit)
 
@@ -353,7 +361,6 @@
         ),
         in_specs=[VMEM] * 4,
         out_specs=(VMEM,) * 4,
-        compiler_params=pltpu.CompilerParams(vmem_limit_bytes=12 << 20),
         name="prepare",
     )(h_frac, h_shift, v_frac, v_shift)
 
@@ -372,9 +379,8 @@
             pltpu.VMEM((fields * rows, BLOCK), jnp.float32),
             pltpu.SemaphoreType.DMA((PAIRS,)),
         ],
-        compiler_params=pltpu.CompilerParams(vmem_limit_bytes=24 << 20),
         name="advect",
-    )(landing, keep_near(got.reshape(-1, BLOCK)), *[keep_near(p) for p in prepared])
+    )(landing, keep_near(got.reshape(-1, BLOCK)), *prepared)
 
 
 def per_device(

time: 136 us -> 130 us (0.956)
  local copies, waits for them, and re-layouts: 14 us -> 0.01 us
  Pallas kernels: 19.5 us -> 26.4 us
  waiting for transfers between devices: 71.5 us -> 75.7 us
  starting transfers between devices: 29.4 us -> 25.8 us
    unnamed x40 -> x2, local copies, waits for them, and re-layouts: 14 us -> 0.01 us
    all_to_all x2, waiting for transfers between devices: 71.5 us -> 75.7 us  [exchange(): return lax.all_to_all(value, AXES, split_axis=0, concat_axis=0, tiled=True)]
    all_to_all x2, starting transfers between devices: 29.4 us -> 25.8 us  [exchange(): return lax.all_to_all(value, AXES, split_axis=0, concat_axis=0, tiled=True)]
    pallas_call x1, Pallas kernels: 1.13 us -> 3.17 us  [prepare(): pl.pallas_call(prepare_kernel, out_shape=(jax.ShapeDtypeStruct((4 * units...]
    pallas_call x1, Pallas kernels: 7.02 us -> 8.97 us  [heat(): pl.pallas_call(heat_kernel, out_shape=(jax.ShapeDtypeStruct((rows, BLOCK)...]
  transfers between devices with their start and end apart: 2 -> 2, of which waited for: 1 -> 2; matrix products, arithmetic and copies ran while one was open for 0% -> 1% of each run, Pallas kernels for 6% -> 9%
where the time goes in v2:
time: 130 us; the launch traced here: 129 us
  waiting for transfers between devices  75.7 us (58%)
  Pallas kernels  26.4 us (20%)
  starting transfers between devices  25.8 us (20%)
    all_to_all x2, waiting for transfers between devices, exchange(): return lax.all_to_all(value, AXES, split_axis=0, concat_axis=0, tiled=True)  75.7 us
    all_to_all x2, starting transfers between devices, exchange(): return lax.all_to_all(value, AXES, split_axis=0, concat_axis=0, tiled=True)  25.8 us
    pallas_call x1, Pallas kernels, heat(): pl.pallas_call(heat_kernel, out_shape=(jax.ShapeDtypeStruct((rows, BLOCK)...  8.97 us
    pallas_call x1, Pallas kernels, advect(): pl.pallas_call(advect_kernel, out_shape=jax.ShapeDtypeStruct((fields * ro...  8.42 us
    pallas_call x1, Pallas kernels, pack(): pl.pallas_call(pack_kernel, grid=(PACK_STEPS,), out_shape=jax.ShapeDtypeS...  4.28 us
    pallas_call x1, Pallas kernels, prepare(): pl.pallas_call(prepare_kernel, out_shape=(jax.ShapeDtypeStruct((4 * units...  3.17 us
  transfers between devices with their start and end apart: 2, of which 2 were waited for; matrix products, arithmetic and copies ran while one was open for 1% of the time, Pallas kernels for 9%

profile of v2, /device:TPU:1, one launch (start us, length us, event | category | flops | bytes accessed | tf_op | source)
XLA Modules:
  0.0 129.3 jit_solution(8685103827926978731)
XLA Ops:
  0.6 1.5 %ask.1 = s32[256,128]{1,0:T(8,128)} custom-call(s32[1,256]{1,0:T(1,128)} %bitcast.28, s32[1,256]{1,0:T(1,128)} %unit.1), custom_call_target="tpu_custom_call" | custom-call | tf_op jit(solution)/shard_map/ask/pallas_call | solution.py:323
  2.2 15.6 %all-to-all-start = ((s32[256,1,128]{2,1,0:T(1,128)}), s32[256,1,128]{2,1,0:T(1,128)S(1)}, u32[]{:S(2)}, u32[]{:S(2)}) async-start(s32[256,1,128]{2,1,0:T(1,128)} %bitcast.23), calls=%async_computation | async-start | bytes 262144 | tf_op jit(solution)/shard_map/all_to_all | solution.py:285
  17.8 9.0 %heat.1 = (f32[1024,128]{1,0:T(8,128)}, s32[3072,128]{1,0:T(8,128)S(1)}) custom-call(f32[6144,128]{1,0:T(8,128)} %bitcast.21, s32[8,128]{1,0:T(8,128)} %bitcast.31, bf16[64,768]{1,0:T(8,128)(2,1)} %w_in.1, f32[1,64]{1,0:T(1,128)} %bitcast.35, bf16[64,224]{1,0:T(8,128)(2,1)} %bitcast.27, f32[1,224]{1,0:T(1,128)} %bitcast.34, f32[224,128]{1,0:T(8,128)} %bitcast.26), custom_call_target="tpu_custom_call" | custom-call | tf_op jit(solution)/shard_map/heat/pallas_call | solution.py:292
  26.8 3.6 %all-to-all-done = s32[256,1,128]{2,1,0:T(1,128)S(1)} async-done(((s32[256,1,128]{2,1,0:T(1,128)}), s32[256,1,128]{2,1,0:T(1,128)S(1)}, u32[]{:S(2)}, u32[]{:S(2)}) %all-to-all-start) | async-done | bytes 131104 | tf_op jit(solution)/shard_map/all_to_all | solution.py:285
  30.4 4.3 %pack.1 = s32[256,24,128]{2,1,0:T(8,128)} custom-call(s32[256,128]{1,0:T(8,128)S(1)} %bitcast.20, s32[3072,128]{1,0:T(8,128)S(1)} %get-tuple-element.8.code), custom_call_target="tpu_custom_call" | custom-call | tf_op jit(solution)/shard_map/pack/pallas_call | solution.py:335
  34.7 0.0 copy-start
  34.7 10.1 %all-to-all-start.1 = ((s32[256,24,128]{2,1,0:T(8,128)}), s32[256,24,128]{2,1,0:T(8,128)S(1)}, u32[]{:S(2)}, u32[]{:S(2)}) async-start(s32[256,24,128]{2,1,0:T(8,128)} %pack.1), calls=%async_computation.1 | async-start | bytes 6291456 | tf_op jit(solution)/shard_map/all_to_all | solution.py:285
  44.8 3.2 %prepare.1 = (f32[1024,128]{1,0:T(8,128)}, s32[1024,128]{1,0:T(8,128)}, bf16[1024,128]{1,0:T(8,128)(2,1)}, bf16[1024,128]{1,0:T(8,128)(2,1)}) custom-call(f32[256,128]{1,0:T(8,128)} %bitcast.24, s32[256,128]{1,0:T(8,128)} %bitcast.25, f32[8,128]{1,0:T(8,128)} %bitcast.32, s32[8,128]{1,0:T(8,128)} %bitcast.33), custom_call_target="tpu_custom_call" | custom-call | tf_op jit(solution)/shard_map/prepare/pallas_call | solution.py:354
  48.0 0.0 copy-done
  48.0 0.2 fusion.1
  48.2 0.6 convert_add_fusion.landing
  48.8 72.1 %all-to-all-done.1 = s32[256,24,128]{2,1,0:T(8,128)S(1)} async-done(((s32[256,24,128]{2,1,0:T(8,128)}), s32[256,24,128]{2,1,0:T(8,128)S(1)}, u32[]{:S(2)}, u32[]{:S(2)}) %all-to-all-start.1) | async-done | bytes 3145760 | tf_op jit(solution)/shard_map/all_to_all | solution.py:285
  120.9 8.4 %advect.1 = f32[6144,128]{1,0:T(8,128)} custom-call(s32[256]{0:T(256)} %convert_add_fusion.landing, s32[6144,128]{1,0:T(8,128)S(1)} %bitcast.19, f32[1024,128]{1,0:T(8,128)} %get-tuple-element.9.weights, s32[1024,128]{1,0:T(8,128)} %get-tuple-element.10.places, bf16[1024,128]{1,0:T(8,128)(2,1)} %get-tuple-element.11.v_high, ...), custom_call_target="tpu_custom_call" | custom-call | tf_op jit(solution)/shard_map/advect/pallas_call | solution.py:372
Async XLA Ops:
  2.2 28.2 %all-to-all-start = ((s32[256,1,128]{2,1,0:T(1,128)}), s32[256,1,128]{2,1,0:T(1,128)S(1)}, u32[]{:S(2)}, u32[]{:S(2)}) async-start(s32[256,1,128]{2,1,0:T(1,128)} %bitcast.23), calls=%async_computation | async-start | bytes 262144 | tf_op jit(solution)/shard_map/all_to_all | solution.py:285
  34.7 13.3 %copy-start = (s32[1,256,1]{1,2,0:T(1,128)S(1)}, s32[1,256,1]{1,2,0:T(1,128)}, u32[]{:S(2)}) copy-start(s32[1,256,1]{1,2,0:T(1,128)} %param.20) | copy-start | bytes 3076
  34.7 86.2 %all-to-all-start.1 = ((s32[256,24,128]{2,1,0:T(8,128)}), s32[256,24,128]{2,1,0:T(8,128)S(1)}, u32[]{:S(2)}, u32[]{:S(2)}) async-start(s32[256,24,128]{2,1,0:T(8,128)} %pack.1), calls=%async_computation.1 | async-start | bytes 6291456 | tf_op jit(solution)/shard_map/all_to_all | solution.py:285

commit v3 on v2

--- a/solution.py
+++ b/solution.py
@@ -12,7 +12,7 @@
 PAIRS = 3
 UNROLL = 16
 VERTICAL_UNROLL = 8
-PACK_STEPS = 8
+PACK_STEPS = 4
 AXES = ("lat", "lon")
 CODE = 16480.0
 SPLIT = 2.0**-75
@@ -122,35 +122,38 @@
     asked[...] = jnp.broadcast_to(low | (high << 16), asked.shape)
 
 
-def pack_kernel(asked, code, sent, row, starts, sem):
-    devices = sent.shape[0]
+def pack_kernel(asked, code, sent, row, starts, built, sem, sems):
+    devices = built.shape[0]
     rows = code.shape[0] // PAIRS
-
-    @pl.when(pl.program_id(0) == 0)
-    def _():
-        diagonal = lax.broadcasted_iota(jnp.int32, (BLOCK, BLOCK), 0) == lax.broadcasted_iota(
-            jnp.int32, (BLOCK, BLOCK), 1
-        )
-        for i in range(asked.shape[0] // BLOCK):
-            tile = jnp.where(diagonal, asked[pl.ds(i * BLOCK, BLOCK), :], 0)
-            row[pl.ds(i, 1), :] = jnp.sum(tile, axis=0, keepdims=True)
-        copy = pltpu.make_async_copy(row, starts, sem)
-        copy.start()
+    diagonal = lax.broadcasted_iota(jnp.int32, (BLOCK, BLOCK), 0) == lax.broadcasted_iota(
+        jnp.int32, (BLOCK, BLOCK), 1
+    )
+    for i in range(devices // BLOCK):
+        tile = jnp.where(diagonal, asked[pl.ds(i * BLOCK, BLOCK), :], 0)
+        row[pl.ds(i, 1), :] = jnp.sum(tile, axis=0, keepdims=True)
+    scalars = pltpu.make_async_copy(row, starts, sem)
+    scalars.start()
+    scalars.wait()
+    part = devices // PACK_STEPS
+    copies = []
+    for step in range(PACK_STEPS):
+        at = (step * part) % BLOCK
+
+        def one(d, carry):
+            both = starts[step * part // BLOCK, at + d]
+            for j, start in enumerate((both & 0xFFFF, both >> 16)):
+                for p in range(PAIRS):
+                    built[step * part + d, pl.ds((j * PAIRS + p) * LG, LG), :] = code[
+                        pl.ds(start + p * rows, LG, stride=8), :
+                    ]
+            return carry
+
+        lax.fori_loop(0, part, one, 0, unroll=16)
+        here = pl.ds(step * part, part)
+        copies.append(pltpu.make_async_copy(built.at[here], sent.at[here], sems.at[step]))
+        copies[-1].start()
+    for copy in copies:
         copy.wait()
-
-    base = pl.program_id(0) * devices
-
-    def one(d, carry):
-        owner = base + d
-        both = starts[owner >> 7, owner & (BLOCK - 1)]
-        for j, at in enumerate((both & 0xFFFF, both >> 16)):
-            for p in range(PAIRS):
-                sent[d, pl.ds((j * PAIRS + p) * LG, LG), :] = code[
-                    pl.ds(at + p * rows, LG, stride=8), :
-                ]
-        return carry
-
-    lax.fori_loop(0, devices, one, 0, unroll=16)
 
 
 def prepare_kernel(h_frac, h_shift, v_frac, v_shift, weights, places, v_high, v_low):
@@ -334,14 +337,15 @@
     shape = (devices, 2 * PAIRS * LG, BLOCK)
     return pl.pallas_call(
         pack_kernel,
-        grid=(PACK_STEPS,),
         out_shape=jax.ShapeDtypeStruct(shape, jnp.int32),
         in_specs=[VMEM] * 2,
-        out_specs=pl.BlockSpec((devices // PACK_STEPS,) + shape[1:], lambda i: (i, 0, 0)),
+        out_specs=ANY,
         scratch_shapes=[
             pltpu.VMEM((devices // BLOCK, BLOCK), jnp.int32),
             pltpu.SMEM((devices // BLOCK, BLOCK), jnp.int32),
+            pltpu.VMEM(shape, jnp.int32),
             pltpu.SemaphoreType.DMA,
+            pltpu.SemaphoreType.DMA((PACK_STEPS,)),
         ],
         compiler_params=pltpu.CompilerParams(vmem_limit_bytes=12 << 20),
         name="pack",

time: 130 us -> 128 us (0.985)
  Pallas kernels: 26.4 us -> 24.6 us
    pallas_call x1, Pallas kernels: 4.28 us -> 2.49 us  [pack(): pl.pallas_call(pack_kernel, out_shape=jax.ShapeDtypeStruct(shape, jnp.int...]
  transfers between devices with their start and end apart: 2 -> 2, of which waited for: 2 -> 2; matrix products, arithmetic and copies ran while one was open for 1% -> 1% of each run, Pallas kernels for 9% -> 10%
where the time goes in v3:
time: 128 us
  waiting for transfers between devices  75.7 us (59%)
  starting transfers between devices  25.8 us (20%)
  Pallas kernels  24.6 us (19%)
    all_to_all x2, waiting for transfers between devices, exchange(): return lax.all_to_all(value, AXES, split_axis=0, concat_axis=0, tiled=True)  75.7 us
    all_to_all x2, starting transfers between devices, exchange(): return lax.all_to_all(value, AXES, split_axis=0, concat_axis=0, tiled=True)  25.8 us
    pallas_call x1, Pallas kernels, heat(): pl.pallas_call(heat_kernel, out_shape=(jax.ShapeDtypeStruct((rows, BLOCK)...  8.97 us
    pallas_call x1, Pallas kernels, advect(): pl.pallas_call(advect_kernel, out_shape=jax.ShapeDtypeStruct((fields * ro...  8.41 us
    pallas_call x1, Pallas kernels, prepare(): pl.pallas_call(prepare_kernel, out_shape=(jax.ShapeDtypeStruct((4 * units...  3.17 us
  transfers between devices with their start and end apart: 2, of which 2 were waited for; matrix products, arithmetic and copies ran while one was open for 1% of the time, Pallas kernels for 10%

profile of v3, /device:TPU:1, one launch (start us, length us, event | category | flops | bytes accessed | tf_op | source)
XLA Modules:
  0.0 127.5 jit_solution(1568402408368077241)
XLA Ops:
  0.6 1.5 %ask.1 = s32[256,128]{1,0:T(8,128)} custom-call(s32[1,256]{1,0:T(1,128)} %bitcast.28, s32[1,256]{1,0:T(1,128)} %unit.1), custom_call_target="tpu_custom_call" | custom-call | tf_op jit(solution)/shard_map/ask/pallas_call | solution.py:326
  2.2 15.6 %all-to-all-start = ((s32[256,1,128]{2,1,0:T(1,128)}), s32[256,1,128]{2,1,0:T(1,128)S(1)}, u32[]{:S(2)}, u32[]{:S(2)}) async-start(s32[256,1,128]{2,1,0:T(1,128)} %bitcast.23), calls=%async_computation | async-start | bytes 262144 | tf_op jit(solution)/shard_map/all_to_all | solution.py:288
  17.8 9.0 %heat.1 = (f32[1024,128]{1,0:T(8,128)}, s32[3072,128]{1,0:T(8,128)S(1)}) custom-call(f32[6144,128]{1,0:T(8,128)} %bitcast.21, s32[8,128]{1,0:T(8,128)} %bitcast.31, bf16[64,768]{1,0:T(8,128)(2,1)} %w_in.1, f32[1,64]{1,0:T(1,128)} %bitcast.35, bf16[64,224]{1,0:T(8,128)(2,1)} %bitcast.27, f32[1,224]{1,0:T(1,128)} %bitcast.34, f32[224,128]{1,0:T(8,128)} %bitcast.26), custom_call_target="tpu_custom_call" | custom-call | tf_op jit(solution)/shard_map/heat/pallas_call | solution.py:295
  26.8 3.6 %all-to-all-done = s32[256,1,128]{2,1,0:T(1,128)S(1)} async-done(((s32[256,1,128]{2,1,0:T(1,128)}), s32[256,1,128]{2,1,0:T(1,128)S(1)}, u32[]{:S(2)}, u32[]{:S(2)}) %all-to-all-start) | async-done | bytes 131104 | tf_op jit(solution)/shard_map/all_to_all | solution.py:288
  30.4 2.5 %pack.1 = s32[256,24,128]{2,1,0:T(8,128)} custom-call(s32[256,128]{1,0:T(8,128)S(1)} %bitcast.20, s32[3072,128]{1,0:T(8,128)S(1)} %get-tuple-element.8.code), custom_call_target="tpu_custom_call" | custom-call | tf_op jit(solution)/shard_map/pack/pallas_call | solution.py:338
  32.9 0.0 copy-start
  32.9 10.1 %all-to-all-start.1 = ((s32[256,24,128]{2,1,0:T(8,128)}), s32[256,24,128]{2,1,0:T(8,128)S(1)}, u32[]{:S(2)}, u32[]{:S(2)}) async-start(s32[256,24,128]{2,1,0:T(8,128)} %pack.1), calls=%async_computation.1 | async-start | bytes 6291456 | tf_op jit(solution)/shard_map/all_to_all | solution.py:288
  43.0 3.2 %prepare.1 = (f32[1024,128]{1,0:T(8,128)}, s32[1024,128]{1,0:T(8,128)}, bf16[1024,128]{1,0:T(8,128)(2,1)}, bf16[1024,128]{1,0:T(8,128)(2,1)}) custom-call(f32[256,128]{1,0:T(8,128)} %bitcast.24, s32[256,128]{1,0:T(8,128)} %bitcast.25, f32[8,128]{1,0:T(8,128)} %bitcast.32, s32[8,128]{1,0:T(8,128)} %bitcast.33), custom_call_target="tpu_custom_call" | custom-call | tf_op jit(solution)/shard_map/prepare/pallas_call | solution.py:358
  46.2 0.0 copy-done
  46.2 0.2 fusion.1
  46.4 0.6 convert_add_fusion.landing
  47.0 72.1 %all-to-all-done.1 = s32[256,24,128]{2,1,0:T(8,128)S(1)} async-done(((s32[256,24,128]{2,1,0:T(8,128)}), s32[256,24,128]{2,1,0:T(8,128)S(1)}, u32[]{:S(2)}, u32[]{:S(2)}) %all-to-all-start.1) | async-done | bytes 3145760 | tf_op jit(solution)/shard_map/all_to_all | solution.py:288
  119.1 8.4 %advect.1 = f32[6144,128]{1,0:T(8,128)} custom-call(s32[256]{0:T(256)} %convert_add_fusion.landing, s32[6144,128]{1,0:T(8,128)S(1)} %bitcast.19, f32[1024,128]{1,0:T(8,128)} %get-tuple-element.9.weights, s32[1024,128]{1,0:T(8,128)} %get-tuple-element.10.places, bf16[1024,128]{1,0:T(8,128)(2,1)} %get-tuple-element.11.v_high, ...), custom_call_target="tpu_custom_call" | custom-call | tf_op jit(solution)/shard_map/advect/pallas_call | solution.py:376
Async XLA Ops:
  2.2 28.2 %all-to-all-start = ((s32[256,1,128]{2,1,0:T(1,128)}), s32[256,1,128]{2,1,0:T(1,128)S(1)}, u32[]{:S(2)}, u32[]{:S(2)}) async-start(s32[256,1,128]{2,1,0:T(1,128)} %bitcast.23), calls=%async_computation | async-start | bytes 262144 | tf_op jit(solution)/shard_map/all_to_all | solution.py:288
  32.9 13.3 %copy-start = (s32[1,256,1]{1,2,0:T(1,128)S(1)}, s32[1,256,1]{1,2,0:T(1,128)}, u32[]{:S(2)}) copy-start(s32[1,256,1]{1,2,0:T(1,128)} %param.20) | copy-start | bytes 3076
  32.9 86.2 %all-to-all-start.1 = ((s32[256,24,128]{2,1,0:T(8,128)}), s32[256,24,128]{2,1,0:T(8,128)S(1)}, u32[]{:S(2)}, u32[]{:S(2)}) async-start(s32[256,24,128]{2,1,0:T(8,128)} %pack.1), calls=%async_computation.1 | async-start | bytes 6291456 | tf_op jit(solution)/shard_map/all_to_all | solution.py:288

commit v4 on v3

--- a/solution.py
+++ b/solution.py
@@ -1,4 +1,4 @@
-import functools
+import math
 
 import jax
 import jax.numpy as jnp
@@ -10,7 +10,7 @@
 BLOCK = 128
 LG = 4
 PAIRS = 3
-UNROLL = 16
+TOGETHER = 4
 VERTICAL_UNROLL = 8
 PACK_STEPS = 4
 AXES = ("lat", "lon")
@@ -40,23 +40,18 @@
 def softplus(v):
     u = jnp.exp(-jnp.abs(v))
     return jnp.maximum(v, 0.0) + jnp.where(
-        u < 0.01, u * (1.0 - u * (0.5 - u * (1.0 / 3.0 - u * 0.25))), jnp.log(1.0 + u)
+        u < 0.005, u * (1.0 - u * (0.5 - u * (1.0 / 3.0))), jnp.log(1.0 + u)
     )
 
 
 def coded(x):
-    root = jnp.exp2(jnp.log2(jnp.abs(x)) * 0.2) * CODE
-    return jnp.where(x < 0.0, -root, root)
-
-
-def nearest(value):
-    return jnp.floor(value + 0.5).astype(jnp.int32)
+    power = jnp.exp2(jnp.log(jnp.maximum(jnp.abs(x), 1e-30)) * (-0.8 / math.log(2.0)) + math.log2(65536.0 * CODE))
+    return (x * power).astype(jnp.int32) + 32768
 
 
 def word_of(first, second):
-    low = nearest(coded(second)) & 0xFFFF
-    high = nearest(coded(first) - low.astype(jnp.float32) * (1.0 / 65536.0))
-    return (high << 16) | low
+    low = lax.shift_right_logical(coded(second), 16)
+    return ((coded(first) - low) & -65536) | low
 
 
 def heat_kernel(x, sun, w_in, b_in, w_out, b_out, level_map, heat, code):
@@ -80,8 +75,7 @@
         hidden = jnp.tanh(mxu(w_in[...], features, 1) + bias_in).astype(jnp.bfloat16)
         optical = softplus(mxu(w_out[...], hidden, 0) + bias_out) * (4.0 / outs)
         high, rest = halves(optical)
-        middle = (optical - high.astype(jnp.float32)) - rest.astype(jnp.float32)
-        depth = mxu(lower, high, 1) + mxu(lower, rest, 1) + mxu(lower, middle.astype(jnp.bfloat16), 1)
+        depth = mxu(lower, high, 1) + mxu(lower, rest, 1)
         high, rest = halves(optical * jnp.exp(-depth))
         warm = mxu(map_high, high, 0) + mxu(map_high, rest, 0) + mxu(map_low, high, 0)
         for i in range(2):
@@ -209,10 +203,8 @@
     fields = 2 * PAIRS
     upper = lax.broadcasted_iota(jnp.int32, (2 * LG, BLOCK), 0) < LG
 
-    def one_block(b, carry):
-        base = b * (fields * levels)
-
-        def two_units(step, inner):
+    def some_blocks(turn, carry):
+        def two_units(step, b, base):
             unit = [(step * 2 + i) * blocks + b for i in range(2)]
             row = [landing[u] * (PAIRS * LG) for u in unit]
             tails = [got[pl.ds(r + LG, 2 * LG), :] for r in row]
@@ -241,12 +233,14 @@
                 f = 2 + half * PAIRS
                 at = pl.multiple_of(base + f * levels + step * 2 * LG, 2 * LG)
                 traced[pl.ds(at, 2 * LG), :] = sums[4 + half]
-            return inner
-
-        lax.fori_loop(0, groups // 2, two_units, 0, unroll=UNROLL)
+
+        for i in range(TOGETHER):
+            b = turn * TOGETHER + i
+            for step in range(groups // 2):
+                two_units(step, b, b * (fields * levels))
         return carry
 
-    lax.fori_loop(0, blocks, one_block, 0)
+    lax.fori_loop(0, blocks // TOGETHER, some_blocks, 0)
     copies = []
     for first in range(0, fields, 2):
 

time: 128 us -> 127 us (level)
  transfers between devices with their start and end apart: 2 -> 2, of which waited for: 2 -> 2; matrix products, arithmetic and copies ran while one was open for 1% -> 1% of each run, Pallas kernels for 10% -> 9%
where the time goes in v4:
time: 127 us; the launch traced here: 126 us
  waiting for transfers between devices  76.4 us (60%)
  starting transfers between devices  25 us (20%)
  Pallas kernels  23.4 us (18%)
    all_to_all x2, waiting for transfers between devices, exchange(): return lax.all_to_all(value, AXES, split_axis=0, concat_axis=0, tiled=True)  76.4 us
    all_to_all x2, starting transfers between devices, exchange(): return lax.all_to_all(value, AXES, split_axis=0, concat_axis=0, tiled=True)  25 us
    pallas_call x1, Pallas kernels, heat(): pl.pallas_call(heat_kernel, out_shape=(jax.ShapeDtypeStruct((rows, BLOCK)...  8.23 us
    pallas_call x1, Pallas kernels, advect(): pl.pallas_call(advect_kernel, out_shape=jax.ShapeDtypeStruct((fields * ro...  7.99 us
    pallas_call x1, Pallas kernels, prepare(): pl.pallas_call(prepare_kernel, out_shape=(jax.ShapeDtypeStruct((4 * units...  3.17 us
  transfers between devices with their start and end apart: 2, of which 2 were waited for; matrix products, arithmetic and copies ran while one was open for 1% of the time, Pallas kernels for 9%

profile of v4, /device:TPU:1, one launch (start us, length us, event | category | flops | bytes accessed | tf_op | source)
XLA Modules:
  0.0 126.4 jit_solution(14680719247896792694)
XLA Ops:
  0.6 1.5 %ask.1 = s32[256,128]{1,0:T(8,128)} custom-call(s32[1,256]{1,0:T(1,128)} %bitcast.28, s32[1,256]{1,0:T(1,128)} %unit.1), custom_call_target="tpu_custom_call" | custom-call | tf_op jit(solution)/shard_map/ask/pallas_call | solution.py:320
  2.2 15.6 %all-to-all-start = ((s32[256,1,128]{2,1,0:T(1,128)}), s32[256,1,128]{2,1,0:T(1,128)S(1)}, u32[]{:S(2)}, u32[]{:S(2)}) async-start(s32[256,1,128]{2,1,0:T(1,128)} %bitcast.23), calls=%async_computation | async-start | bytes 262144 | tf_op jit(solution)/shard_map/all_to_all | solution.py:282
  17.8 8.2 %heat.1 = (f32[1024,128]{1,0:T(8,128)}, s32[3072,128]{1,0:T(8,128)S(1)}) custom-call(f32[6144,128]{1,0:T(8,128)} %bitcast.21, s32[8,128]{1,0:T(8,128)} %bitcast.31, bf16[64,768]{1,0:T(8,128)(2,1)} %w_in.1, f32[1,64]{1,0:T(1,128)} %bitcast.35, bf16[64,224]{1,0:T(8,128)(2,1)} %bitcast.27, f32[1,224]{1,0:T(1,128)} %bitcast.34, f32[224,128]{1,0:T(8,128)} %bitcast.26), custom_call_target="tpu_custom_call" | custom-call | tf_op jit(solution)/shard_map/heat/pallas_call | solution.py:289
  26.0 4.3 %all-to-all-done = s32[256,1,128]{2,1,0:T(1,128)S(1)} async-done(((s32[256,1,128]{2,1,0:T(1,128)}), s32[256,1,128]{2,1,0:T(1,128)S(1)}, u32[]{:S(2)}, u32[]{:S(2)}) %all-to-all-start) | async-done | bytes 131104 | tf_op jit(solution)/shard_map/all_to_all | solution.py:282
  30.4 2.5 %pack.1 = s32[256,24,128]{2,1,0:T(8,128)} custom-call(s32[256,128]{1,0:T(8,128)S(1)} %bitcast.20, s32[3072,128]{1,0:T(8,128)S(1)} %get-tuple-element.8.code), custom_call_target="tpu_custom_call" | custom-call | tf_op jit(solution)/shard_map/pack/pallas_call | solution.py:332
  32.9 0.0 copy-start
  32.9 9.4 %all-to-all-start.1 = ((s32[256,24,128]{2,1,0:T(8,128)}), s32[256,24,128]{2,1,0:T(8,128)S(1)}, u32[]{:S(2)}, u32[]{:S(2)}) async-start(s32[256,24,128]{2,1,0:T(8,128)} %pack.1), calls=%async_computation.1 | async-start | bytes 6291456 | tf_op jit(solution)/shard_map/all_to_all | solution.py:282
  42.3 3.2 %prepare.1 = (f32[1024,128]{1,0:T(8,128)}, s32[1024,128]{1,0:T(8,128)}, bf16[1024,128]{1,0:T(8,128)(2,1)}, bf16[1024,128]{1,0:T(8,128)(2,1)}) custom-call(f32[256,128]{1,0:T(8,128)} %bitcast.24, s32[256,128]{1,0:T(8,128)} %bitcast.25, f32[8,128]{1,0:T(8,128)} %bitcast.32, s32[8,128]{1,0:T(8,128)} %bitcast.33), custom_call_target="tpu_custom_call" | custom-call | tf_op jit(solution)/shard_map/prepare/pallas_call | solution.py:352
  45.5 0.0 copy-done
  45.5 0.2 fusion.1
  45.6 0.6 convert_add_fusion.landing
  46.2 72.1 %all-to-all-done.1 = s32[256,24,128]{2,1,0:T(8,128)S(1)} async-done(((s32[256,24,128]{2,1,0:T(8,128)}), s32[256,24,128]{2,1,0:T(8,128)S(1)}, u32[]{:S(2)}, u32[]{:S(2)}) %all-to-all-start.1) | async-done | bytes 3145760 | tf_op jit(solution)/shard_map/all_to_all | solution.py:282
  118.4 8.0 %advect.1 = f32[6144,128]{1,0:T(8,128)} custom-call(s32[256]{0:T(256)} %convert_add_fusion.landing, s32[6144,128]{1,0:T(8,128)S(1)} %bitcast.19, f32[1024,128]{1,0:T(8,128)} %get-tuple-element.9.weights, s32[1024,128]{1,0:T(8,128)} %get-tuple-element.10.places, bf16[1024,128]{1,0:T(8,128)(2,1)} %get-tuple-element.11.v_high, ...), custom_call_target="tpu_custom_call" | custom-call | tf_op jit(solution)/shard_map/advect/pallas_call | solution.py:370
Async XLA Ops:
  2.2 28.2 %all-to-all-start = ((s32[256,1,128]{2,1,0:T(1,128)}), s32[256,1,128]{2,1,0:T(1,128)S(1)}, u32[]{:S(2)}, u32[]{:S(2)}) async-start(s32[256,1,128]{2,1,0:T(1,128)} %bitcast.23), calls=%async_computation | async-start | bytes 262144 | tf_op jit(solution)/shard_map/all_to_all | solution.py:282
  32.9 12.6 %copy-start = (s32[1,256,1]{1,2,0:T(1,128)S(1)}, s32[1,256,1]{1,2,0:T(1,128)}, u32[]{:S(2)}) copy-start(s32[1,256,1]{1,2,0:T(1,128)} %param.20) | copy-start | bytes 3076
  32.9 85.5 %all-to-all-start.1 = ((s32[256,24,128]{2,1,0:T(8,128)}), s32[256,24,128]{2,1,0:T(8,128)S(1)}, u32[]{:S(2)}, u32[]{:S(2)}) async-start(s32[256,24,128]{2,1,0:T(8,128)} %pack.1), calls=%async_computation.1 | async-start | bytes 6291456 | tf_op jit(solution)/shard_map/all_to_all | solution.py:282

commit v5 on v4

--- a/solution.py
+++ b/solution.py
@@ -10,7 +10,7 @@
 BLOCK = 128
 LG = 4
 PAIRS = 3
-TOGETHER = 4
+TOGETHER = 8
 VERTICAL_UNROLL = 8
 PACK_STEPS = 4
 AXES = ("lat", "lon")
@@ -142,7 +142,7 @@
                     ]
             return carry
 
-        lax.fori_loop(0, part, one, 0, unroll=16)
+        lax.fori_loop(0, part, one, 0, unroll=32)
         here = pl.ds(step * part, part)
         copies.append(pltpu.make_async_copy(built.at[here], sent.at[here], sems.at[step]))
         copies[-1].start()

time: 127 us -> 126 us (level)
  no operation moved by 1% of the time
where the time goes in v5:
time: 126 us
  waiting for transfers between devices  76.4 us (61%)
  starting transfers between devices  25 us (20%)
  Pallas kernels  23.1 us (18%)
    all_to_all x2, waiting for transfers between devices, exchange(): return lax.all_to_all(value, AXES, split_axis=0, concat_axis=0, tiled=True)  76.4 us
    all_to_all x2, starting transfers between devices, exchange(): return lax.all_to_all(value, AXES, split_axis=0, concat_axis=0, tiled=True)  25 us
    pallas_call x1, Pallas kernels, heat(): pl.pallas_call(heat_kernel, out_shape=(jax.ShapeDtypeStruct((rows, BLOCK)...  8.23 us
    pallas_call x1, Pallas kernels, advect(): pl.pallas_call(advect_kernel, out_shape=jax.ShapeDtypeStruct((fields * ro...  7.69 us
    pallas_call x1, Pallas kernels, prepare(): pl.pallas_call(prepare_kernel, out_shape=(jax.ShapeDtypeStruct((4 * units...  3.17 us
  transfers between devices with their start and end apart: 2, of which 2 were waited for; matrix products, arithmetic and copies ran while one was open for 1% of the time, Pallas kernels for 9%

profile of v5, /device:TPU:1, one launch (start us, length us, event | category | flops | bytes accessed | tf_op | source)
XLA Modules:
  0.0 126.1 jit_solution(5943557406707810970)
XLA Ops:
  0.6 1.5 %ask.1 = s32[256,128]{1,0:T(8,128)} custom-call(s32[1,256]{1,0:T(1,128)} %bitcast.28, s32[1,256]{1,0:T(1,128)} %unit.1), custom_call_target="tpu_custom_call" | custom-call | tf_op jit(solution)/shard_map/ask/pallas_call | solution.py:320
  2.2 15.6 %all-to-all-start = ((s32[256,1,128]{2,1,0:T(1,128)}), s32[256,1,128]{2,1,0:T(1,128)S(1)}, u32[]{:S(2)}, u32[]{:S(2)}) async-start(s32[256,1,128]{2,1,0:T(1,128)} %bitcast.23), calls=%async_computation | async-start | bytes 262144 | tf_op jit(solution)/shard_map/all_to_all | solution.py:282
  17.8 8.2 %heat.1 = (f32[1024,128]{1,0:T(8,128)}, s32[3072,128]{1,0:T(8,128)S(1)}) custom-call(f32[6144,128]{1,0:T(8,128)} %bitcast.21, s32[8,128]{1,0:T(8,128)} %bitcast.31, bf16[64,768]{1,0:T(8,128)(2,1)} %w_in.1, f32[1,64]{1,0:T(1,128)} %bitcast.35, bf16[64,224]{1,0:T(8,128)(2,1)} %bitcast.27, f32[1,224]{1,0:T(1,128)} %bitcast.34, f32[224,128]{1,0:T(8,128)} %bitcast.26), custom_call_target="tpu_custom_call" | custom-call | tf_op jit(solution)/shard_map/heat/pallas_call | solution.py:289
  26.0 4.3 %all-to-all-done = s32[256,1,128]{2,1,0:T(1,128)S(1)} async-done(((s32[256,1,128]{2,1,0:T(1,128)}), s32[256,1,128]{2,1,0:T(1,128)S(1)}, u32[]{:S(2)}, u32[]{:S(2)}) %all-to-all-start) | async-done | bytes 131104 | tf_op jit(solution)/shard_map/all_to_all | solution.py:282
  30.4 2.5 %pack.1 = s32[256,24,128]{2,1,0:T(8,128)} custom-call(s32[256,128]{1,0:T(8,128)S(1)} %bitcast.20, s32[3072,128]{1,0:T(8,128)S(1)} %get-tuple-element.8.code), custom_call_target="tpu_custom_call" | custom-call | tf_op jit(solution)/shard_map/pack/pallas_call | solution.py:332
  32.9 0.0 copy-start
  32.9 9.4 %all-to-all-start.1 = ((s32[256,24,128]{2,1,0:T(8,128)}), s32[256,24,128]{2,1,0:T(8,128)S(1)}, u32[]{:S(2)}, u32[]{:S(2)}) async-start(s32[256,24,128]{2,1,0:T(8,128)} %pack.1), calls=%async_computation.1 | async-start | bytes 6291456 | tf_op jit(solution)/shard_map/all_to_all | solution.py:282
  42.3 3.2 %prepare.1 = (f32[1024,128]{1,0:T(8,128)}, s32[1024,128]{1,0:T(8,128)}, bf16[1024,128]{1,0:T(8,128)(2,1)}, bf16[1024,128]{1,0:T(8,128)(2,1)}) custom-call(f32[256,128]{1,0:T(8,128)} %bitcast.24, s32[256,128]{1,0:T(8,128)} %bitcast.25, f32[8,128]{1,0:T(8,128)} %bitcast.32, s32[8,128]{1,0:T(8,128)} %bitcast.33), custom_call_target="tpu_custom_call" | custom-call | tf_op jit(solution)/shard_map/prepare/pallas_call | solution.py:352
  45.4 0.0 copy-done
  45.5 0.2 fusion.1
  45.6 0.6 convert_add_fusion.landing
  46.2 72.1 %all-to-all-done.1 = s32[256,24,128]{2,1,0:T(8,128)S(1)} async-done(((s32[256,24,128]{2,1,0:T(8,128)}), s32[256,24,128]{2,1,0:T(8,128)S(1)}, u32[]{:S(2)}, u32[]{:S(2)}) %all-to-all-start.1) | async-done | bytes 3145760 | tf_op jit(solution)/shard_map/all_to_all | solution.py:282
  118.4 7.7 %advect.1 = f32[6144,128]{1,0:T(8,128)} custom-call(s32[256]{0:T(256)} %convert_add_fusion.landing, s32[6144,128]{1,0:T(8,128)S(1)} %bitcast.19, f32[1024,128]{1,0:T(8,128)} %get-tuple-element.9.weights, s32[1024,128]{1,0:T(8,128)} %get-tuple-element.10.places, bf16[1024,128]{1,0:T(8,128)(2,1)} %get-tuple-element.11.v_high, ...), custom_call_target="tpu_custom_call" | custom-call | tf_op jit(solution)/shard_map/advect/pallas_call | solution.py:370
Async XLA Ops:
  2.2 28.2 %all-to-all-start = ((s32[256,1,128]{2,1,0:T(1,128)}), s32[256,1,128]{2,1,0:T(1,128)S(1)}, u32[]{:S(2)}, u32[]{:S(2)}) async-start(s32[256,1,128]{2,1,0:T(1,128)} %bitcast.23), calls=%async_computation | async-start | bytes 262144 | tf_op jit(solution)/shard_map/all_to_all | solution.py:282
  32.9 12.6 %copy-start = (s32[1,256,1]{1,2,0:T(1,128)S(1)}, s32[1,256,1]{1,2,0:T(1,128)}, u32[]{:S(2)}) copy-start(s32[1,256,1]{1,2,0:T(1,128)} %param.20) | copy-start | bytes 3076
  32.9 85.5 %all-to-all-start.1 = ((s32[256,24,128]{2,1,0:T(8,128)}), s32[256,24,128]{2,1,0:T(8,128)S(1)}, u32[]{:S(2)}, u32[]{:S(2)}) async-start(s32[256,24,128]{2,1,0:T(8,128)} %pack.1), calls=%async_computation.1 | async-start | bytes 6291456 | tf_op jit(solution)/shard_map/all_to_all | solution.py:282
